TPU v7x, 32 devices: a whole 2x2x4 slice. The times are simulated.
32 devices in a mesh: layer: 2 (over y), feat: 4 (over x, core), width: 4 (over z).
Axes of the slice: x: 2, y: 2, z: 4, core: 2. Of those that a mesh axis runs over, the one named last changes fastest.
Arguments:
- resid: bfloat16 [2, 128, 2048], P(None, 'layer', 'width'), may hold values from -6 to 6
- enc_w: bfloat16 [2, 2048, 65536], P(None, 'width', ('layer', 'feat')), may hold values from -0.125 to 0.125
- enc_b: float32 [2, 65536], P(None, ('layer', 'feat')), may hold values from -3 to 3
- dec_w: float32 [3, 65536, 2048], P(None, ('layer', 'feat'), 'width'), may hold values from -0.03125 to 0.03125
- dec_b: float32 [2, 2048], P(None, 'width'), may hold values from -2 to 2
- target: float32 [2, 128, 2048], P(None, ('layer', 'feat'), 'width'), may hold values from -6 to 6
Outputs:
- recon: float32 [2, 128, 2048], P(None, ('layer', 'feat'), 'width')
- err: float32 [2, 128], P(None, ('layer', 'feat'))
All inputs are finite; a program needn't handle non-finite values.
Results may differ from a plain program's by a relative error of at most 0.00035.
Values may be sent and summed in bfloat16 or wider, within the bound.
No kernel may reach another device: no remote copies, remote signals or barrier semaphores. Data moves between devices by JAX's collectives and lax.ppermute only.
A program may use at most 128 MiB of HBM per device.

v0:
```python
import jax
import jax.numpy as jnp
from jax import lax
from jax.sharding import PartitionSpec as P


def decode_rows(act, dec_w, target_idx):
    total = None
    for layer_idx in range(target_idx + 1):
        block = target_idx * (target_idx + 1) // 2 + layer_idx
        rows = act[layer_idx]
        term = jnp.dot(
            rows, dec_w[block], precision=lax.Precision.HIGHEST, preferred_element_type=jnp.float32
        )
        total = term if total is None else total + term
    return total


def per_device(resid, enc_w, enc_b, dec_w, dec_b, target):
    layers = resid.shape[0]
    gathered = lax.all_gather(resid, "layer", axis=1, tiled=True)
    tokens = gathered.shape[1]
    partial_pre = jnp.einsum("ltd,ldf->ltf", gathered, enc_w, preferred_element_type=jnp.float32)
    pre = lax.psum(partial_pre, "width")
    act = jnp.maximum(pre + enc_b[:, None, :], 0.0)
    own_rows = tokens // lax.axis_size(("layer", "feat"))
    summed = lax.psum_scatter(
        jnp.concatenate(
            [decode_rows(act, dec_w, target_idx) for target_idx in range(layers)], axis=1
        ),
        ("layer", "feat"),
        scatter_dimension=0,
        tiled=True,
    )
    summed = summed.reshape(own_rows, layers, dec_w.shape[2]).transpose(1, 0, 2)
    recon = summed + dec_b[:, None, :]
    diff = recon - target
    sq_error, sq_target = lax.psum(
        (jnp.sum(diff * diff, axis=2), jnp.sum(target * target, axis=2)), "width"
    )
    err = sq_error / (sq_target + 1e-06)
    return (recon, err)


def solution(mesh):
    in_specs = (
        P(None, "layer", "width"),
        P(None, "width", ("layer", "feat")),
        P(None, ("layer", "feat")),
        P(None, ("layer", "feat"), "width"),
        P(None, "width"),
        P(None, ("layer", "feat"), "width"),
    )
    out_specs = (P(None, ("layer", "feat"), "width"), P(None, ("layer", "feat")))
    return jax.shard_map(
        per_device, mesh=mesh, in_specs=in_specs, out_specs=out_specs, check_vma=False
    )
```

profile of v0, /device:TPU:0, one launch (start us, length us, event | category | flops | bytes accessed | tf_op | source)
XLA Modules:
  0.0 413.2 jit_solution(15221711624656479680)
XLA Ops:
  7.2 0.0 all-reduce.3.cloned.1.call-start
  7.2 7.4 %all_gather.3 = bf16[2,128,512]{2,1,0:T(8,128)(2,1)S(1)} all-gather(bf16[2,64,512]{2,1,0:T(8,128)(2,1)} %param.6), channel_id=1, replica_groups=mesh['layer'=2,'feat'=4,'width'=4] {'layer'}, dimensions={1}, use_global_device_ids=true | all-gather | bytes 393216 | tf_op jit(solution)/shard_map/all_gather | solution.py:21
  14.6 11.3 %fusion.14 = f32[2,128,8192]{2,1,0:T(8,128)} fusion(bf16[2,128,512]{2,1,0:T(8,128)(2,1)S(1)} %all_gather.3, bf16[2,512,8192]{2,1,0:T(8,128)(2,1)} %param.7), kind=kOutput, calls=%fused_computation.19 | convolution fusion | flops 2147483648 | bytes 25427968 | tf_op jit(solution)/shard_map/ltd,ldf->ltf/dot_general | solution.py:23
  26.0 0.0 copy-start
  26.0 0.0 all-reduce.3.cloned.1.call-update
  26.0 0.0 reduce-scatter.2.cloned.1.call-start
  26.0 292.4 %all-reduce.3.cloned.1.call-done = f32[2,128,8192]{2,1,0:T(8,128)} async-done(((f32[2,128,8192]{2,1,0:T(8,128)}), f32[2,128,8192]{2,1,0:T(8,128)}) %all-reduce.3.cloned.1.call-update) | async-done | bytes 8388624 | tf_op jit(solution)/shard_map/psum | solution.py:24
  318.4 0.0 copy-done
  318.4 4.2 %add_maximum_fusion = f32[2,128,8192]{2,1,0:T(8,128)S(1)} fusion(f32[2,128,8192]{2,1,0:T(8,128)} %all-reduce.3.cloned.1.call-done, f32[2,8192]{1,0:T(2,128)S(1)} %copy-done), kind=kLoop, calls=%fused_computation.9 | loop fusion | flops 4194304 | bytes 16842752 | tf_op jit(solution)/shard_map/max | solution.py:25
  322.6 11.9 %fusion = f32[128,512]{1,0:T(8,128)S(1)} fusion(f32[3,8192,512]{2,1,0:T(8,128)} %param.9, f32[2,128,8192]{2,1,0:T(8,128)S(1)} %add_maximum_fusion), kind=kOutput, calls=%fused_computation | convolution fusion | flops 6442450944 | bytes 21233664 | tf_op jit(solution)/shard_map/dot_general | solution.py:12
  334.5 11.9 %fusion.4 = f32[128,512]{1,0:T(8,128)S(1)} fusion(f32[3,8192,512]{2,1,0:T(8,128)} %param.9, f32[2,128,8192]{2,1,0:T(8,128)S(1)} %add_maximum_fusion), kind=kOutput, calls=%fused_computation.4 | convolution fusion | flops 6442450944 | bytes 21233664 | tf_op jit(solution)/shard_map/dot_general | solution.py:12
  346.4 0.0 copy-start.1
  346.4 0.0 copy-start.2
  346.4 12.1 %fusion.9 = f32[128,512]{1,0:T(8,128)S(1)} fusion(f32[128,512]{1,0:T(8,128)S(1)} %fusion, f32[3,8192,512]{2,1,0:T(8,128)} %param.9, f32[2,128,8192]{2,1,0:T(8,128)S(1)} %add_maximum_fusion), kind=kOutput, calls=%fused_computation.12 | convolution fusion | flops 6442516480 | bytes 21495808 | tf_op jit(solution)/shard_map/dot_general | solution.py:12
  358.5 0.8 pad_maximum_fusion
  359.3 0.0 reduce-scatter.2.cloned.1.call-update
  359.4 33.2 %reduce-scatter.2.cloned.1.call-done = f32[16,1024]{1,0:T(8,128)} async-done(((f32[128,1024]{1,0:T(8,128)}), f32[16,1024]{1,0:T(8,128)}) %reduce-scatter.2.cloned.1.call-update) | async-done | bytes 65552 | tf_op jit(solution)/shard_map/reduce_scatter | solution.py:27
  392.6 0.0 copy-done.1
  392.6 0.0 copy-done.2
  392.6 1.5 multiply_reduce_fusion
  394.1 11.6 %all-reduce = (f32[2,16]{1,0:T(2,128)S(1)}, f32[2,16]{1,0:T(2,128)S(1)}) all-reduce(f32[2,16]{1,0:T(2,128)S(1)} %get-tuple-element.3, f32[2,16]{1,0:T(2,128)S(1)} %get-tuple-element.2), channel_id=1, replica_groups=mesh['layer'=2,'feat'=4,'width'=4] {'width'}, use_global_device_ids=true, to_apply=%region_3.0 | all-reduce | flops 64 | bytes 512 | tf_op jit(solution)/shard_map/psum | solution.py:38
  405.8 0.6 add_divide_fusion
Async XLA Ops:
  7.2 311.2 %all-reduce.3.cloned.1.call-start = ((), (), s32[]{:S(2)}) async-start(), calls=%async_computation.1 | async-start | bytes 16777216 | tf_op jit(solution)/shard_map/psum | solution.py:24
  26.0 292.4 %copy-start = (f32[2,8192]{1,0:T(2,128)S(1)}, f32[2,8192]{1,0:T(2,128)}, u32[]{:S(2)}) copy-start(f32[2,8192]{1,0:T(2,128)} %param.8) | copy-start | bytes 196612
  26.0 366.6 %reduce-scatter.2.cloned.1.call-start = ((), (), s32[]{:S(2)}) async-start(), calls=%async_computation.2 | async-start | bytes 589824 | tf_op jit(solution)/shard_map/reduce_scatter | solution.py:27
  346.4 46.2 %copy-start.1 = (f32[2,16,512]{2,1,0:T(8,128)S(1)}, f32[2,16,512]{2,1,0:T(8,128)}, u32[]{:S(2)}) copy-start(f32[2,16,512]{2,1,0:T(8,128)} %param.11) | copy-start | bytes 196612
  346.4 46.2 %copy-start.2 = (f32[2,512]{1,0:T(2,128)S(1)}, f32[2,512]{1,0:T(2,128)}, u32[]{:S(2)}) copy-start(f32[2,512]{1,0:T(2,128)} %param.10) | copy-start | bytes 12292
Sparse Core Ops, SparseCore 0:
  26.1 292.2 all-reduce.2
  359.5 33.0 reduce-scatter.1
where the time goes:
time: 413 us
  waiting for transfers between devices  326 us (79%)
  matrix products  47.2 us (11%)
  blocking collectives  19.1 us (5%)
  between operations  14.1 us (3%)
  other arithmetic  7.07 us (2%)
    psum x1, waiting for transfers between devices, per_device(): pre = lax.psum(partial_pre, 'width')  292 us
    dot_general x3, matrix products, decode_rows(): jnp.dot(rows, dec_w[block], precision=lax.Precision.HIGHEST, preferred_el...  35.9 us
    reduce_scatter x1, waiting for transfers between devices, per_device(): lax.psum_scatter(jnp.concatenate([decode_rows(act, dec_w, target_idx) for...  33.2 us
    psum x1, blocking collectives, per_device(): lax.psum((jnp.sum(diff * diff, axis=2), jnp.sum(target * target, axis=2))...  11.6 us
    dot_general x1, matrix products, per_device(): jnp.einsum('ltd,ldf->ltf', gathered, enc_w, preferred_element_type=jnp.fl...  11.3 us
  transfers between devices with their start and end apart: 2, of which 2 were waited for; matrix products, arithmetic and copies ran while one was open for 0% of the time, Pallas kernels for 0%

commit v1 on v0

v1 whole, which is shorter than its diff:
```python
import math

import jax
import jax.numpy as jnp
from jax import lax
from jax.sharding import PartitionSpec as P

RESID_MAX = 6.0
ENC_MAX = 0.125
F16_MAX = 65504.0


def chunk_bounds(features, parts):
    unit = features // sum(parts)
    bounds, start = [], 0
    for part in parts:
        bounds.append((start, start + part * unit))
        start += part * unit
    return bounds


def halving(rows, axis):
    size = lax.axis_size(axis)
    me = lax.axis_index(axis)
    bit = 1
    blocks = rows.reshape((size, rows.shape[0] // size) + rows.shape[1:])
    count = size
    while count > 1:
        pairs = blocks.reshape((count // 2, 2) + blocks.shape[1:])
        mine = (me // bit) % 2
        keep = lax.dynamic_index_in_dim(pairs, mine, 1, keepdims=False)
        give = lax.dynamic_index_in_dim(pairs, 1 - mine, 1, keepdims=False)
        got = lax.ppermute(give, axis, [(i, i ^ bit) for i in range(size)])
        blocks = keep + got
        bit *= 2
        count //= 2
    return blocks[0]


def butterfly(value, axis):
    size = lax.axis_size(axis)
    bit = 1
    while bit < size:
        value = value + lax.ppermute(value, axis, [(i, i ^ bit) for i in range(size)])
        bit *= 2
    return value


def gather_tokens(resid, axis):
    size = lax.axis_size(axis)
    if size != 2:
        return lax.all_gather(resid, axis, axis=1, tiled=True)
    other = lax.ppermute(resid, axis, [(0, 1), (1, 0)])
    first = lax.axis_index(axis) == 0
    return jnp.concatenate(
        [jnp.where(first, resid, other), jnp.where(first, other, resid)], axis=1
    )


def per_device(resid, enc_w, enc_b, dec_w, dec_b, target):
    layers, _, width = resid.shape
    features = enc_w.shape[2]
    size = lax.axis_size("width")
    scale = 2.0 ** math.floor(math.log2(F16_MAX / (width * size * RESID_MAX * ENC_MAX)))
    gathered = gather_tokens(resid, "layer") * jnp.asarray(scale, resid.dtype)
    tokens = gathered.shape[1]

    work = []
    for layer in range(layers):
        parts = (1, 1, 2, 2, 2) if layer == 0 else (2, 2, 2, 1, 1)
        work += [(layer, lo, hi) for lo, hi in chunk_bounds(features, parts)]

    partial, received = [], []
    for layer, lo, hi in work:
        partial.append(
            jnp.dot(gathered[layer], enc_w[layer, :, lo:hi], preferred_element_type=jnp.float32)
        )
        received.append({})

    def exchange(k, j):
        value = partial[k]
        if j > 1:
            value = value + received[k][j - 1].astype(jnp.float32)
        received[k][j] = lax.ppermute(
            value.astype(jnp.float16), "width", [(j - 1, j), (size - j, size - j - 1)]
        )

    count = len(work)
    for stage in range(count + size - 2):
        for j in range(1, size):
            if 0 <= stage - j + 1 < count:
                exchange(stage - j + 1, j)

    recon = [None] * layers
    for k, (layer, lo, hi) in enumerate(work):
        total = partial[k]
        for j in range(1, size):
            total = total + received[k][j].astype(jnp.float32)
        act = jnp.maximum(total + scale * enc_b[layer, lo:hi], 0.0)
        for m in range(layer, layers):
            block = m * (m + 1) // 2 + layer
            term = jnp.dot(
                act, dec_w[block, lo:hi], precision=lax.Precision.HIGH,
                preferred_element_type=jnp.float32,
            )
            recon[m] = term if recon[m] is None else recon[m] + term

    outs, errs = [], []
    for m in range(layers):
        rows = recon[m].reshape(lax.axis_size("layer"), -1, recon[m].shape[1])
        rows = rows.transpose(1, 0, 2)
        rows = halving(rows, "feat").transpose(1, 0, 2)
        rows = halving(rows.reshape((-1,) + rows.shape[2:]), "layer")
        out = rows * (1.0 / scale) + dec_b[m]
        diff = out - target[m]
        sums = jnp.stack([jnp.sum(diff * diff, axis=1), jnp.sum(target[m] * target[m], axis=1)])
        sums = butterfly(sums, "width")
        outs.append(out)
        errs.append(sums[0] / (sums[1] + 1e-06))
    return jnp.stack(outs), jnp.stack(errs)


def solution(mesh):
    in_specs = (
        P(None, "layer", "width"),
        P(None, "width", ("layer", "feat")),
        P(None, ("layer", "feat")),
        P(None, ("layer", "feat"), "width"),
        P(None, "width"),
        P(None, ("layer", "feat"), "width"),
    )
    out_specs = (P(None, ("layer", "feat"), "width"), P(None, ("layer", "feat")))
    return jax.shard_map(
        per_device, mesh=mesh, in_specs=in_specs, out_specs=out_specs, check_vma=False
    )
```

time: 413 us -> 279 us (0.68)
  waiting for transfers between devices: 326 us -> 138 us
  starting transfers between devices: 0.08 us -> 65.4 us
  blocking collectives: 19.1 us -> 0 us
  matrix products: 47.2 us -> 65.9 us
  between operations: 14.1 us -> 1.58 us
    psum x1 -> x0, waiting for transfers between devices: 292 us -> none  [per_device(): pre = lax.psum(partial_pre, 'width')]
    ppermute x0 -> x41, waiting for transfers between devices: none -> 138 us  [the longest x30 125 us: exchange(): lax.ppermute(value.astype(jnp.float16), 'width', [(j - 1, j), (size - j,...]
    ppermute x0 -> x41, starting transfers between devices: none -> 65.4 us  [the longest x30 50.7 us: exchange(): lax.ppermute(value.astype(jnp.float16), 'width', [(j - 1, j), (size - j,...]
    reduce_scatter x1 -> x0, waiting for transfers between devices: 33.2 us -> none  [per_device(): lax.psum_scatter(jnp.concatenate([decode_rows(act, dec_w, target_idx) for...]
    dot_general x4 -> x25, matrix products: 47.2 us -> 65.9 us  [the longest x15 47.5 us: per_device(): jnp.dot(act, dec_w[block, lo:hi], precision=lax.Precision.HIGH, preferred...]
    psum x1 -> x0, blocking collectives: 11.6 us -> none  [per_device(): lax.psum((jnp.sum(diff * diff, axis=2), jnp.sum(target * target, axis=2))...]
    all_gather x1 -> x0, blocking collectives: 7.42 us -> none  [per_device(): gathered = lax.all_gather(resid, 'layer', axis=1, tiled=True)]
    max x1 -> x0, other arithmetic: 4.19 us -> none  [per_device(): act = jnp.maximum(pre + enc_b[:, None, :], 0.0)]
  transfers between devices with their start and end apart: 2 -> 41, of which waited for: 2 -> 21; matrix products, arithmetic and copies ran while one was open for 0% -> 18% of each run, Pallas kernels for 0% -> 0%
where the time goes in v1:
time: 279 us; the launch traced here: 278 us
  waiting for transfers between devices  138 us (49%)
  matrix products  65.9 us (24%)
  starting transfers between devices  65.4 us (23%)
  other arithmetic  6.36 us (2%)
    ppermute x30, waiting for transfers between devices, exchange(): lax.ppermute(value.astype(jnp.float16), 'width', [(j - 1, j), (size - j,...  125 us
    ppermute x30, starting transfers between devices, exchange(): lax.ppermute(value.astype(jnp.float16), 'width', [(j - 1, j), (size - j,...  50.7 us
    dot_general x15, matrix products, per_device(): jnp.dot(act, dec_w[block, lo:hi], precision=lax.Precision.HIGH, preferred...  47.5 us
    dot_general x10, matrix products, per_device(): jnp.dot(gathered[layer], enc_w[layer, :, lo:hi], preferred_element_type=j...  18.4 us
    ppermute x4, starting transfers between devices, butterfly(): lax.ppermute(value, axis, [(i, i ^ bit) for i in range(size)])  6.01 us
    ppermute x6, waiting for transfers between devices, halving(): got = lax.ppermute(give, axis, [(i, i ^ bit) for i in range(size)])  5.7 us
    ppermute x6, starting transfers between devices, halving(): got = lax.ppermute(give, axis, [(i, i ^ bit) for i in range(size)])  5.68 us
  transfers between devices with their start and end apart: 41, of which 21 were waited for; matrix products, arithmetic and copies ran while one was open for 18% of the time, Pallas kernels for 0%

profile of v1, /device:TPU:0, one launch (start us, length us, event | category | flops | bytes accessed | tf_op | source)
XLA Modules:
  0.0 277.5 jit_solution(12963653236721281802)
XLA Ops:
  0.6 3.1 %collective-permute-start = (bf16[2,64,512]{2,1,0:T(8,128)(2,1)}, bf16[2,64,512]{2,1,0:T(8,128)(2,1)S(1)}, u32[]{:S(2)}, u32[]{:S(2)}) collective-permute-start(bf16[2,64,512]{2,1,0:T(8,128)(2,1)} %param.6), channel_id=1, source_target_pairs={{0,16},{16,0},{1,17},{17,1},{2,18},{18,2},{3,19},{19,3},{4,20},{20... | collective-permute-start | bytes 393224 | tf_op jit(solution)/shard_map/ppermute | solution.py:53
  5.3 2.1 collective-permute-done
  8.4 1.5 fusion.219
  9.9 1.5 fusion.210
  11.5 1.5 fusion.217
  13.0 2.0 fusion.212
  15.1 2.0 fusion.211
  17.1 2.0 fusion.216
  19.2 2.0 fusion.215
  21.2 2.0 fusion.214
  23.2 2.0 fusion.213
  25.3 3.7 %collective-permute-start.28 = (f16[128,1024]{1,0:T(8,128)(2,1)S(1)}, f16[128,1024]{1,0:T(8,128)(2,1)S(1)}, u32[]{:S(2)}, u32[]{:S(2)}) collective-permute-start(f16[128,1024]{1,0:T(8,128)(2,1)S(1)} %get-tuple-element.42), channel_id=1, source_target_pairs={{0,1},{3,2},{4,5},{7,6},{8,9},{11,10},{12,13},{15,14},{16,17},{19,... | collective-permute-start | bytes 786440 | tf_op jit(solution)/shard_map/ppermute | solution.py:84
  29.0 1.3 collective-permute-start.31
  30.3 1.5 fusion.218
  31.9 1.3 collective-permute-start.4
  33.2 1.3 collective-permute-start.1
  34.5 1.3 collective-permute-start.22
  35.8 4.2 %collective-permute-start.25 = (f16[128,2048]{1,0:T(8,128)(2,1)S(1)}, f16[128,2048]{1,0:T(8,128)(2,1)S(1)}, u32[]{:S(2)}, u32[]{:S(2)}) collective-permute-start(f16[128,2048]{1,0:T(8,128)(2,1)S(1)} %get-tuple-element.26), channel_id=1, source_target_pairs={{0,1},{3,2},{4,5},{7,6},{8,9},{11,10},{12,13},{15,14},{16,17},{19,... | collective-permute-start | bytes 1572872 | tf_op jit(solution)/shard_map/ppermute | solution.py:84
  41.3 4.4 %collective-permute-start.7 = (f16[128,2048]{1,0:T(8,128)(2,1)S(1)}, f16[128,2048]{1,0:T(8,128)(2,1)S(1)}, u32[]{:S(2)}, u32[]{:S(2)}) collective-permute-start(f16[128,2048]{1,0:T(8,128)(2,1)S(1)} %get-tuple-element.36), channel_id=1, source_target_pairs={{0,1},{3,2},{4,5},{7,6},{8,9},{11,10},{12,13},{15,14},{16,17},{19,... | collective-permute-start | bytes 1572872 | tf_op jit(solution)/shard_map/ppermute | solution.py:84
  46.9 4.4 %collective-permute-start.10 = (f16[128,2048]{1,0:T(8,128)(2,1)S(1)}, f16[128,2048]{1,0:T(8,128)(2,1)S(1)}, u32[]{:S(2)}, u32[]{:S(2)}) collective-permute-start(f16[128,2048]{1,0:T(8,128)(2,1)S(1)} %get-tuple-element.34), channel_id=1, source_target_pairs={{0,1},{3,2},{4,5},{7,6},{8,9},{11,10},{12,13},{15,14},{16,17},{19,... | collective-permute-start | bytes 1572872 | tf_op jit(solution)/shard_map/ppermute | solution.py:84
  52.5 4.4 %collective-permute-start.13 = (f16[128,2048]{1,0:T(8,128)(2,1)S(1)}, f16[128,2048]{1,0:T(8,128)(2,1)S(1)}, u32[]{:S(2)}, u32[]{:S(2)}) collective-permute-start(f16[128,2048]{1,0:T(8,128)(2,1)S(1)} %get-tuple-element.32), channel_id=1, source_target_pairs={{0,1},{3,2},{4,5},{7,6},{8,9},{11,10},{12,13},{15,14},{16,17},{19,... | collective-permute-start | bytes 1572872 | tf_op jit(solution)/shard_map/ppermute | solution.py:84
  57.0 6.7 %collective-permute-done.22 = f16[128,2048]{1,0:T(8,128)(2,1)S(1)} collective-permute-done((f16[128,2048]{1,0:T(8,128)(2,1)S(1)}, f16[128,2048]{1,0:T(8,128)(2,1)S(1)}, u32[]{:S(2)}, u32[]{:S(2)}) %collective-permute-start.22) | collective-permute-done | bytes 524320 | tf_op jit(solution)/shard_map/ppermute | solution.py:84
  63.8 4.4 %collective-permute-start.19 = (f16[128,2048]{1,0:T(8,128)(2,1)S(1)}, f16[128,2048]{1,0:T(8,128)(2,1)S(1)}, u32[]{:S(2)}, u32[]{:S(2)}) collective-permute-start(f16[128,2048]{1,0:T(8,128)(2,1)S(1)} %get-tuple-element.30), channel_id=1, source_target_pairs={{0,1},{3,2},{4,5},{7,6},{8,9},{11,10},{12,13},{15,14},{16,17},{19,... | collective-permute-start | bytes 1572872 | tf_op jit(solution)/shard_map/ppermute | solution.py:84
  68.3 6.7 %collective-permute-done.25 = f16[128,2048]{1,0:T(8,128)(2,1)S(1)} collective-permute-done((f16[128,2048]{1,0:T(8,128)(2,1)S(1)}, f16[128,2048]{1,0:T(8,128)(2,1)S(1)}, u32[]{:S(2)}, u32[]{:S(2)}) %collective-permute-start.25) | collective-permute-done | bytes 524320 | tf_op jit(solution)/shard_map/ppermute | solution.py:84
  75.8 10.4 %collective-permute-done.7 = f16[128,2048]{1,0:T(8,128)(2,1)S(1)} collective-permute-done((f16[128,2048]{1,0:T(8,128)(2,1)S(1)}, f16[128,2048]{1,0:T(8,128)(2,1)S(1)}, u32[]{:S(2)}, u32[]{:S(2)}) %collective-permute-start.7) | collective-permute-done | bytes 524320 | tf_op jit(solution)/shard_map/ppermute | solution.py:84
  87.1 10.4 %collective-permute-done.10 = f16[128,2048]{1,0:T(8,128)(2,1)S(1)} collective-permute-done((f16[128,2048]{1,0:T(8,128)(2,1)S(1)}, f16[128,2048]{1,0:T(8,128)(2,1)S(1)}, u32[]{:S(2)}, u32[]{:S(2)}) %collective-permute-start.10) | collective-permute-done | bytes 524320 | tf_op jit(solution)/shard_map/ppermute | solution.py:84
  99.1 1.3 collective-permute-start.30
  100.5 1.3 collective-permute-start.33
  101.9 1.3 collective-permute-start.6
  103.3 5.5 %collective-permute-done.13 = f16[128,2048]{1,0:T(8,128)(2,1)S(1)} collective-permute-done((f16[128,2048]{1,0:T(8,128)(2,1)S(1)}, f16[128,2048]{1,0:T(8,128)(2,1)S(1)}, u32[]{:S(2)}, u32[]{:S(2)}) %collective-permute-start.13) | collective-permute-done | bytes 524320 | tf_op jit(solution)/shard_map/ppermute | solution.py:84
  110.1 7.8 %collective-permute-done.19 = f16[128,2048]{1,0:T(8,128)(2,1)S(1)} collective-permute-done((f16[128,2048]{1,0:T(8,128)(2,1)S(1)}, f16[128,2048]{1,0:T(8,128)(2,1)S(1)}, u32[]{:S(2)}, u32[]{:S(2)}) %collective-permute-start.19) | collective-permute-done | bytes 524320 | tf_op jit(solution)/shard_map/ppermute | solution.py:84
  118.8 4.6 %collective-permute-done.6 = f16[128,1024]{1,0:T(8,128)(2,1)S(1)} collective-permute-done((f16[128,1024]{1,0:T(8,128)(2,1)S(1)}, f16[128,1024]{1,0:T(8,128)(2,1)S(1)}, u32[]{:S(2)}, u32[]{:S(2)}) %collective-permute-start.6) | collective-permute-done | bytes 262176 | tf_op jit(solution)/shard_map/ppermute | solution.py:84
  124.1 2.4 fusion.37
  126.5 2.4 fusion.47
  129.6 2.4 fusion.27
  134.6 1.3 collective-permute-start.24
  136.0 1.3 collective-permute-start.9
  137.5 1.3 collective-permute-start.27
  138.9 52.2 %collective-permute-done.9 = f16[128,2048]{1,0:T(8,128)(2,1)S(1)} collective-permute-done((f16[128,2048]{1,0:T(8,128)(2,1)S(1)}, f16[128,2048]{1,0:T(8,128)(2,1)S(1)}, u32[]{:S(2)}, u32[]{:S(2)}) %collective-permute-start.9) | collective-permute-done | bytes 524320 | tf_op jit(solution)/shard_map/ppermute | solution.py:84
  191.1 1.5 collective-permute-start.12
  192.6 3.7 %fusion.10 = f32[128,512]{1,0:T(8,128)S(1)} fusion(f32[3,8192,512]{2,1,0:T(8,128)} %param.9, f16[128,2048]{1,0:T(8,128)(2,1)S(1)} %collective-permute-done.8, f16[128,2048]{1,0:T(8,128)(2,1)S(1)} %collective-permute-done.9, f32[128,2048]{1,0:T(8,128)S(1)} %get-tuple-element.37, f16[128,2048]{1,0:T(8,128)(2,1)S(1)} %collective-permute-done.7, ...), kind=kOutput, calls=%fused_computation.10 | convolution fusion | flops 807403520 | bytes 7086080 | tf_op jit(solution)/shard_map/dot_general | solution.py:102
  196.3 3.7 %fusion.16 = f32[128,512]{1,0:T(8,128)S(1)} fusion(f32[3,8192,512]{2,1,0:T(8,128)} %param.9, f16[128,2048]{1,0:T(8,128)(2,1)S(1)} %collective-permute-done.8, f16[128,2048]{1,0:T(8,128)(2,1)S(1)} %collective-permute-done.9, f32[128,2048]{1,0:T(8,128)S(1)} %get-tuple-element.37, f16[128,2048]{1,0:T(8,128)(2,1)S(1)} %collective-permute-done.7, ...), kind=kOutput, calls=%fused_computation.16 | convolution fusion | flops 807403520 | bytes 7086080 | tf_op jit(solution)/shard_map/dot_general | solution.py:102
  200.0 13.0 %collective-permute-done.12 = f16[128,2048]{1,0:T(8,128)(2,1)S(1)} collective-permute-done((f16[128,2048]{1,0:T(8,128)(2,1)S(1)}, f16[128,2048]{1,0:T(8,128)(2,1)S(1)}, u32[]{:S(2)}, u32[]{:S(2)}) %collective-permute-start.12) | collective-permute-done | bytes 524320 | tf_op jit(solution)/shard_map/ppermute | solution.py:84
  213.0 1.3 collective-permute-start.15
  214.2 3.7 %fusion.8 = f32[128,512]{1,0:T(8,128)S(1)} fusion(f32[3,8192,512]{2,1,0:T(8,128)} %param.9, f16[128,2048]{1,0:T(8,128)(2,1)S(1)} %collective-permute-done.11, f16[128,2048]{1,0:T(8,128)(2,1)S(1)} %collective-permute-done.12, f32[128,2048]{1,0:T(8,128)S(1)} %get-tuple-element.35, f16[128,2048]{1,0:T(8,128)(2,1)S(1)} %collective-permute-done.10, ...), kind=kOutput, calls=%fused_computation.8 | convolution fusion | flops 807403520 | bytes 7086080 | tf_op jit(solution)/shard_map/dot_general | solution.py:102
  217.9 3.7 %fusion.14 = f32[128,512]{1,0:T(8,128)S(1)} fusion(f32[3,8192,512]{2,1,0:T(8,128)} %param.9, f16[128,2048]{1,0:T(8,128)(2,1)S(1)} %collective-permute-done.11, f16[128,2048]{1,0:T(8,128)(2,1)S(1)} %collective-permute-done.12, f32[128,2048]{1,0:T(8,128)S(1)} %get-tuple-element.35, f16[128,2048]{1,0:T(8,128)(2,1)S(1)} %collective-permute-done.10, ...), kind=kOutput, calls=%fused_computation.14 | convolution fusion | flops 807403520 | bytes 7086080 | tf_op jit(solution)/shard_map/dot_general | solution.py:102
  221.6 4.4 %collective-permute-done.15 = f16[128,2048]{1,0:T(8,128)(2,1)S(1)} collective-permute-done((f16[128,2048]{1,0:T(8,128)(2,1)S(1)}, f16[128,2048]{1,0:T(8,128)(2,1)S(1)}, u32[]{:S(2)}, u32[]{:S(2)}) %collective-permute-start.15) | collective-permute-done | bytes 524320 | tf_op jit(solution)/shard_map/ppermute | solution.py:84
  227.3 3.7 %fusion.6 = f32[128,512]{1,0:T(8,128)S(1)} fusion(f32[3,8192,512]{2,1,0:T(8,128)} %param.9, f16[128,2048]{1,0:T(8,128)(2,1)S(1)} %collective-permute-done.14, f16[128,2048]{1,0:T(8,128)(2,1)S(1)} %collective-permute-done.15, f32[128,2048]{1,0:T(8,128)S(1)} %get-tuple-element.33, f16[128,2048]{1,0:T(8,128)(2,1)S(1)} %collective-permute-done.13, ...), kind=kOutput, calls=%fused_computation.6 | convolution fusion | flops 807403520 | bytes 7086080 | tf_op jit(solution)/shard_map/dot_general | solution.py:102
  231.0 3.7 %fusion.12 = f32[128,512]{1,0:T(8,128)S(1)} fusion(f32[3,8192,512]{2,1,0:T(8,128)} %param.9, f16[128,2048]{1,0:T(8,128)(2,1)S(1)} %collective-permute-done.14, f16[128,2048]{1,0:T(8,128)(2,1)S(1)} %collective-permute-done.15, f32[128,2048]{1,0:T(8,128)S(1)} %get-tuple-element.33, f16[128,2048]{1,0:T(8,128)(2,1)S(1)} %collective-permute-done.13, ...), kind=kOutput, calls=%fused_computation.12 | convolution fusion | flops 807403520 | bytes 7086080 | tf_op jit(solution)/shard_map/dot_general | solution.py:102
  234.7 3.7 %fusion.2 = f32[128,512]{1,0:T(8,128)S(1)} fusion(f32[3,8192,512]{2,1,0:T(8,128)} %param.9, f16[128,2048]{1,0:T(8,128)(2,1)S(1)} %collective-permute-done.23, f16[128,2048]{1,0:T(8,128)(2,1)S(1)} %collective-permute-done.24, f32[128,2048]{1,0:T(8,128)S(1)} %get-tuple-element.29, f16[128,2048]{1,0:T(8,128)(2,1)S(1)} %collective-permute-done.22, ...), kind=kOutput, calls=%fused_computation.2 | convolution fusion | flops 807403520 | bytes 7086080 | tf_op jit(solution)/shard_map/dot_general | solution.py:102
  238.4 3.7 %fusion = f32[128,512]{1,0:T(8,128)S(1)} fusion(f32[3,8192,512]{2,1,0:T(8,128)} %param.9, f16[128,2048]{1,0:T(8,128)(2,1)S(1)} %collective-permute-done.26, f16[128,2048]{1,0:T(8,128)(2,1)S(1)} %collective-permute-done.27, f32[128,2048]{1,0:T(8,128)S(1)} %get-tuple-element.27, f16[128,2048]{1,0:T(8,128)(2,1)S(1)} %collective-permute-done.25, ...), kind=kOutput, calls=%fused_computation | convolution fusion | flops 807403520 | bytes 7086080 | tf_op jit(solution)/shard_map/dot_general | solution.py:102
  242.1 3.7 %fusion.4 = f32[128,512]{1,0:T(8,128)S(1)} fusion(f32[3,8192,512]{2,1,0:T(8,128)} %param.9, f16[128,2048]{1,0:T(8,128)(2,1)S(1)} %collective-permute-done.20, f16[128,2048]{1,0:T(8,128)(2,1)S(1)} %collective-permute-done.21, f32[128,2048]{1,0:T(8,128)S(1)} %get-tuple-element.31, f16[128,2048]{1,0:T(8,128)(2,1)S(1)} %collective-permute-done.19, ...), kind=kOutput, calls=%fused_computation.4 | convolution fusion | flops 807403520 | bytes 7086080 | tf_op jit(solution)/shard_map/dot_general | solution.py:102
  245.8 2.5 fusion.93
  248.3 2.4 fusion.99
  250.7 2.4 fusion.78
  254.6 1.6 collective-permute-start.17
  256.8 2.3 collective-permute-done.17
  259.2 1.6 collective-permute-start.18
  260.8 1.4 collective-permute-start.36
  263.2 1.6 collective-permute-done.36
  265.0 2.7 collective-permute-start.39
  269.3 3.1 %collective-permute-start.40 = (f32[2,16]{1,0:T(2,128)S(1)}, f32[2,16]{1,0:T(2,128)S(1)}, u32[]{:S(2)}, u32[]{:S(2)}) collective-permute-start(f32[2,16]{1,0:T(2,128)S(1)} %fusion.197), channel_id=1, source_target_pairs={{0,2},{1,3},{2,0},{3,1},{4,6},{5,7},{6,4},{7,5},{8,10},{9,11},{10,... | collective-permute-start | bytes 392 | tf_op jit(solution)/shard_map/ppermute | solution.py:44
  272.5 1.4 collective-permute-done.40
  274.0 3.0 %collective-permute-done.38 = f32[2,16]{1,0:T(2,128)S(1)} collective-permute-done((f32[2,16]{1,0:T(2,128)S(1)}, f32[2,16]{1,0:T(2,128)S(1)}, u32[]{:S(2)}, u32[]{:S(2)}) %collective-permute-start.38) | collective-permute-done | bytes 160 | tf_op jit(solution)/shard_map/ppermute | solution.py:44
  (96 shorter events, 23.1 us)
Async XLA Ops:
  0.6 6.8 %collective-permute-start = (bf16[2,64,512]{2,1,0:T(8,128)(2,1)}, bf16[2,64,512]{2,1,0:T(8,128)(2,1)S(1)}, u32[]{:S(2)}, u32[]{:S(2)}) collective-permute-start(bf16[2,64,512]{2,1,0:T(8,128)(2,1)} %param.6), channel_id=1, source_target_pairs={{0,16},{16,0},{1,17},{17,1},{2,18},{18,2},{3,19},{19,3},{4,20},{20... | collective-permute-start | bytes 393224 | tf_op jit(solution)/shard_map/ppermute | solution.py:53
  25.3 10.5 %collective-permute-start.28 = (f16[128,1024]{1,0:T(8,128)(2,1)S(1)}, f16[128,1024]{1,0:T(8,128)(2,1)S(1)}, u32[]{:S(2)}, u32[]{:S(2)}) collective-permute-start(f16[128,1024]{1,0:T(8,128)(2,1)S(1)} %get-tuple-element.42), channel_id=1, source_target_pairs={{0,1},{3,2},{4,5},{7,6},{8,9},{11,10},{12,13},{15,14},{16,17},{19,... | collective-permute-start | bytes 786440 | tf_op jit(solution)/shard_map/ppermute | solution.py:84
  29.0 12.3 %collective-permute-start.31 = (f16[128,1024]{1,0:T(8,128)(2,1)S(1)}, f16[128,1024]{1,0:T(8,128)(2,1)S(1)}, u32[]{:S(2)}, u32[]{:S(2)}) collective-permute-start(f16[128,1024]{1,0:T(8,128)(2,1)S(1)} %get-tuple-element.24), channel_id=1, source_target_pairs={{0,1},{3,2},{4,5},{7,6},{8,9},{11,10},{12,13},{15,14},{16,17},{19,... | collective-permute-start | bytes 786440 | tf_op jit(solution)/shard_map/ppermute | solution.py:84
  31.9 15.0 %collective-permute-start.4 = (f16[128,1024]{1,0:T(8,128)(2,1)S(1)}, f16[128,1024]{1,0:T(8,128)(2,1)S(1)}, u32[]{:S(2)}, u32[]{:S(2)}) collective-permute-start(f16[128,1024]{1,0:T(8,128)(2,1)S(1)} %get-tuple-element.38), channel_id=1, source_target_pairs={{0,1},{3,2},{4,5},{7,6},{8,9},{11,10},{12,13},{15,14},{16,17},{19,... | collective-permute-start | bytes 786440 | tf_op jit(solution)/shard_map/ppermute | solution.py:84
  33.2 19.3 %collective-permute-start.1 = (f16[128,1024]{1,0:T(8,128)(2,1)S(1)}, f16[128,1024]{1,0:T(8,128)(2,1)S(1)}, u32[]{:S(2)}, u32[]{:S(2)}) collective-permute-start(f16[128,1024]{1,0:T(8,128)(2,1)S(1)} %get-tuple-element.40), channel_id=1, source_target_pairs={{0,1},{3,2},{4,5},{7,6},{8,9},{11,10},{12,13},{15,14},{16,17},{19,... | collective-permute-start | bytes 786440 | tf_op jit(solution)/shard_map/ppermute | solution.py:84
  34.5 29.3 %collective-permute-start.22 = (f16[128,2048]{1,0:T(8,128)(2,1)S(1)}, f16[128,2048]{1,0:T(8,128)(2,1)S(1)}, u32[]{:S(2)}, u32[]{:S(2)}) collective-permute-start(f16[128,2048]{1,0:T(8,128)(2,1)S(1)} %get-tuple-element.28), channel_id=1, source_target_pairs={{0,1},{3,2},{4,5},{7,6},{8,9},{11,10},{12,13},{15,14},{16,17},{19,... | collective-permute-start | bytes 1572872 | tf_op jit(solution)/shard_map/ppermute | solution.py:84
  35.8 39.2 %collective-permute-start.25 = (f16[128,2048]{1,0:T(8,128)(2,1)S(1)}, f16[128,2048]{1,0:T(8,128)(2,1)S(1)}, u32[]{:S(2)}, u32[]{:S(2)}) collective-permute-start(f16[128,2048]{1,0:T(8,128)(2,1)S(1)} %get-tuple-element.26), channel_id=1, source_target_pairs={{0,1},{3,2},{4,5},{7,6},{8,9},{11,10},{12,13},{15,14},{16,17},{19,... | collective-permute-start | bytes 1572872 | tf_op jit(solution)/shard_map/ppermute | solution.py:84
  41.3 44.9 %collective-permute-start.7 = (f16[128,2048]{1,0:T(8,128)(2,1)S(1)}, f16[128,2048]{1,0:T(8,128)(2,1)S(1)}, u32[]{:S(2)}, u32[]{:S(2)}) collective-permute-start(f16[128,2048]{1,0:T(8,128)(2,1)S(1)} %get-tuple-element.36), channel_id=1, source_target_pairs={{0,1},{3,2},{4,5},{7,6},{8,9},{11,10},{12,13},{15,14},{16,17},{19,... | collective-permute-start | bytes 1572872 | tf_op jit(solution)/shard_map/ppermute | solution.py:84
  46.9 50.6 %collective-permute-start.10 = (f16[128,2048]{1,0:T(8,128)(2,1)S(1)}, f16[128,2048]{1,0:T(8,128)(2,1)S(1)}, u32[]{:S(2)}, u32[]{:S(2)}) collective-permute-start(f16[128,2048]{1,0:T(8,128)(2,1)S(1)} %get-tuple-element.34), channel_id=1, source_target_pairs={{0,1},{3,2},{4,5},{7,6},{8,9},{11,10},{12,13},{15,14},{16,17},{19,... | collective-permute-start | bytes 1572872 | tf_op jit(solution)/shard_map/ppermute | solution.py:84
  52.5 56.2 %collective-permute-start.13 = (f16[128,2048]{1,0:T(8,128)(2,1)S(1)}, f16[128,2048]{1,0:T(8,128)(2,1)S(1)}, u32[]{:S(2)}, u32[]{:S(2)}) collective-permute-start(f16[128,2048]{1,0:T(8,128)(2,1)S(1)} %get-tuple-element.32), channel_id=1, source_target_pairs={{0,1},{3,2},{4,5},{7,6},{8,9},{11,10},{12,13},{15,14},{16,17},{19,... | collective-permute-start | bytes 1572872 | tf_op jit(solution)/shard_map/ppermute | solution.py:84
  63.8 54.2 %collective-permute-start.19 = (f16[128,2048]{1,0:T(8,128)(2,1)S(1)}, f16[128,2048]{1,0:T(8,128)(2,1)S(1)}, u32[]{:S(2)}, u32[]{:S(2)}) collective-permute-start(f16[128,2048]{1,0:T(8,128)(2,1)S(1)} %get-tuple-element.30), channel_id=1, source_target_pairs={{0,1},{3,2},{4,5},{7,6},{8,9},{11,10},{12,13},{15,14},{16,17},{19,... | collective-permute-start | bytes 1572872 | tf_op jit(solution)/shard_map/ppermute | solution.py:84
  75.0 23.3 %collective-permute-start.29 = (f16[128,1024]{1,0:T(8,128)(2,1)S(1)}, f16[128,1024]{1,0:T(8,128)(2,1)S(1)}, u32[]{:S(2)}, u32[]{:S(2)}) collective-permute-start(f16[128,1024]{1,0:T(8,128)(2,1)S(1)} %fusion.178), channel_id=1, source_target_pairs={{1,2},{2,1},{5,6},{6,5},{9,10},{10,9},{13,14},{14,13},{17,18},{18,... | collective-permute-start | bytes 786440 | tf_op jit(solution)/shard_map/ppermute | solution.py:84
  86.2 12.8 %collective-permute-start.32 = (f16[128,1024]{1,0:T(8,128)(2,1)S(1)}, f16[128,1024]{1,0:T(8,128)(2,1)S(1)}, u32[]{:S(2)}, u32[]{:S(2)}) collective-permute-start(f16[128,1024]{1,0:T(8,128)(2,1)S(1)} %fusion.179), channel_id=1, source_target_pairs={{1,2},{2,1},{5,6},{6,5},{9,10},{10,9},{13,14},{14,13},{17,18},{18,... | collective-permute-start | bytes 786440 | tf_op jit(solution)/shard_map/ppermute | solution.py:84
  97.5 3.0 %collective-permute-start.5 = (f16[128,1024]{1,0:T(8,128)(2,1)S(1)}, f16[128,1024]{1,0:T(8,128)(2,1)S(1)}, u32[]{:S(2)}, u32[]{:S(2)}) collective-permute-start(f16[128,1024]{1,0:T(8,128)(2,1)S(1)} %fusion.177), channel_id=1, source_target_pairs={{1,2},{2,1},{5,6},{6,5},{9,10},{10,9},{13,14},{14,13},{17,18},{18,... | collective-permute-start | bytes 786440 | tf_op jit(solution)/shard_map/ppermute | solution.py:84
  98.3 3.6 %collective-permute-start.2 = (f16[128,1024]{1,0:T(8,128)(2,1)S(1)}, f16[128,1024]{1,0:T(8,128)(2,1)S(1)}, u32[]{:S(2)}, u32[]{:S(2)}) collective-permute-start(f16[128,1024]{1,0:T(8,128)(2,1)S(1)} %fusion.176), channel_id=1, source_target_pairs={{1,2},{2,1},{5,6},{6,5},{9,10},{10,9},{13,14},{14,13},{17,18},{18,... | collective-permute-start | bytes 786440 | tf_op jit(solution)/shard_map/ppermute | solution.py:84
  99.1 151.6 %collective-permute-start.30 = (f16[128,1024]{1,0:T(8,128)(2,1)S(1)}, f16[128,1024]{1,0:T(8,128)(2,1)S(1)}, u32[]{:S(2)}, u32[]{:S(2)}) collective-permute-start(f16[128,1024]{1,0:T(8,128)(2,1)S(1)} %fusion.162), channel_id=1, source_target_pairs={{2,3},{1,0},{6,7},{5,4},{10,11},{9,8},{14,15},{13,12},{18,19},{17,... | collective-permute-start | bytes 786440 | tf_op jit(solution)/shard_map/ppermute | solution.py:84
  100.5 28.4 %collective-permute-start.33 = (f16[128,1024]{1,0:T(8,128)(2,1)S(1)}, f16[128,1024]{1,0:T(8,128)(2,1)S(1)}, u32[]{:S(2)}, u32[]{:S(2)}) collective-permute-start(f16[128,1024]{1,0:T(8,128)(2,1)S(1)} %fusion.167), channel_id=1, source_target_pairs={{2,3},{1,0},{6,7},{5,4},{10,11},{9,8},{14,15},{13,12},{18,19},{17,... | collective-permute-start | bytes 786440 | tf_op jit(solution)/shard_map/ppermute | solution.py:84
  101.9 21.5 %collective-permute-start.6 = (f16[128,1024]{1,0:T(8,128)(2,1)S(1)}, f16[128,1024]{1,0:T(8,128)(2,1)S(1)}, u32[]{:S(2)}, u32[]{:S(2)}) collective-permute-start(f16[128,1024]{1,0:T(8,128)(2,1)S(1)} %fusion.157), channel_id=1, source_target_pairs={{2,3},{1,0},{6,7},{5,4},{10,11},{9,8},{14,15},{13,12},{18,19},{17,... | collective-permute-start | bytes 786440 | tf_op jit(solution)/shard_map/ppermute | solution.py:84
  108.7 137.1 %collective-permute-start.3 = (f16[128,1024]{1,0:T(8,128)(2,1)S(1)}, f16[128,1024]{1,0:T(8,128)(2,1)S(1)}, u32[]{:S(2)}, u32[]{:S(2)}) collective-permute-start(f16[128,1024]{1,0:T(8,128)(2,1)S(1)} %fusion.153), channel_id=1, source_target_pairs={{2,3},{1,0},{6,7},{5,4},{10,11},{9,8},{14,15},{13,12},{18,19},{17,... | collective-permute-start | bytes 786440 | tf_op jit(solution)/shard_map/ppermute | solution.py:84
  118.0 14.0 %collective-permute-start.23 = (f16[128,2048]{1,0:T(8,128)(2,1)S(1)}, f16[128,2048]{1,0:T(8,128)(2,1)S(1)}, u32[]{:S(2)}, u32[]{:S(2)}) collective-permute-start(f16[128,2048]{1,0:T(8,128)(2,1)S(1)} %fusion.148), channel_id=1, source_target_pairs={{1,2},{2,1},{5,6},{6,5},{9,10},{10,9},{13,14},{14,13},{17,18},{18,... | collective-permute-start | bytes 1572872 | tf_op jit(solution)/shard_map/ppermute | solution.py:84
  123.4 9.4 %collective-permute-start.26 = (f16[128,2048]{1,0:T(8,128)(2,1)S(1)}, f16[128,2048]{1,0:T(8,128)(2,1)S(1)}, u32[]{:S(2)}, u32[]{:S(2)}) collective-permute-start(f16[128,2048]{1,0:T(8,128)(2,1)S(1)} %fusion.149), channel_id=1, source_target_pairs={{1,2},{2,1},{5,6},{6,5},{9,10},{10,9},{13,14},{14,13},{17,18},{18,... | collective-permute-start | bytes 1572872 | tf_op jit(solution)/shard_map/ppermute | solution.py:84
  128.9 4.8 %collective-permute-start.8 = (f16[128,2048]{1,0:T(8,128)(2,1)S(1)}, f16[128,2048]{1,0:T(8,128)(2,1)S(1)}, u32[]{:S(2)}, u32[]{:S(2)}) collective-permute-start(f16[128,2048]{1,0:T(8,128)(2,1)S(1)} %fusion.144), channel_id=1, source_target_pairs={{1,2},{2,1},{5,6},{6,5},{9,10},{10,9},{13,14},{14,13},{17,18},{18,... | collective-permute-start | bytes 1572872 | tf_op jit(solution)/shard_map/ppermute | solution.py:84
  132.0 2.6 collective-permute-start.11
  132.9 3.2 %collective-permute-start.14 = (f16[128,2048]{1,0:T(8,128)(2,1)S(1)}, f16[128,2048]{1,0:T(8,128)(2,1)S(1)}, u32[]{:S(2)}, u32[]{:S(2)}) collective-permute-start(f16[128,2048]{1,0:T(8,128)(2,1)S(1)} %fusion.146), channel_id=1, source_target_pairs={{1,2},{2,1},{5,6},{6,5},{9,10},{10,9},{13,14},{14,13},{17,18},{18,... | collective-permute-start | bytes 1572872 | tf_op jit(solution)/shard_map/ppermute | solution.py:84
  133.7 3.7 %collective-permute-start.20 = (f16[128,2048]{1,0:T(8,128)(2,1)S(1)}, f16[128,2048]{1,0:T(8,128)(2,1)S(1)}, u32[]{:S(2)}, u32[]{:S(2)}) collective-permute-start(f16[128,2048]{1,0:T(8,128)(2,1)S(1)} %fusion.147), channel_id=1, source_target_pairs={{1,2},{2,1},{5,6},{6,5},{9,10},{10,9},{13,14},{14,13},{17,18},{18,... | collective-permute-start | bytes 1572872 | tf_op jit(solution)/shard_map/ppermute | solution.py:84
  134.6 100.1 %collective-permute-start.24 = (f16[128,2048]{1,0:T(8,128)(2,1)S(1)}, f16[128,2048]{1,0:T(8,128)(2,1)S(1)}, u32[]{:S(2)}, u32[]{:S(2)}) collective-permute-start(f16[128,2048]{1,0:T(8,128)(2,1)S(1)} %fusion.123), channel_id=1, source_target_pairs={{2,3},{1,0},{6,7},{5,4},{10,11},{9,8},{14,15},{13,12},{18,19},{17,... | collective-permute-start | bytes 1572872 | tf_op jit(solution)/shard_map/ppermute | solution.py:84
  136.0 55.1 %collective-permute-start.9 = (f16[128,2048]{1,0:T(8,128)(2,1)S(1)}, f16[128,2048]{1,0:T(8,128)(2,1)S(1)}, u32[]{:S(2)}, u32[]{:S(2)}) collective-permute-start(f16[128,2048]{1,0:T(8,128)(2,1)S(1)} %fusion.105), channel_id=1, source_target_pairs={{2,3},{1,0},{6,7},{5,4},{10,11},{9,8},{14,15},{13,12},{18,19},{17,... | collective-permute-start | bytes 1572872 | tf_op jit(solution)/shard_map/ppermute | solution.py:84
  137.5 100.9 %collective-permute-start.27 = (f16[128,2048]{1,0:T(8,128)(2,1)S(1)}, f16[128,2048]{1,0:T(8,128)(2,1)S(1)}, u32[]{:S(2)}, u32[]{:S(2)}) collective-permute-start(f16[128,2048]{1,0:T(8,128)(2,1)S(1)} %fusion.128), channel_id=1, source_target_pairs={{2,3},{1,0},{6,7},{5,4},{10,11},{9,8},{14,15},{13,12},{18,19},{17,... | collective-permute-start | bytes 1572872 | tf_op jit(solution)/shard_map/ppermute | solution.py:84
  191.1 21.8 %collective-permute-start.12 = (f16[128,2048]{1,0:T(8,128)(2,1)S(1)}, f16[128,2048]{1,0:T(8,128)(2,1)S(1)}, u32[]{:S(2)}, u32[]{:S(2)}) collective-permute-start(f16[128,2048]{1,0:T(8,128)(2,1)S(1)} %fusion.109), channel_id=1, source_target_pairs={{2,3},{1,0},{6,7},{5,4},{10,11},{9,8},{14,15},{13,12},{18,19},{17,... | collective-permute-start | bytes 1572872 | tf_op jit(solution)/shard_map/ppermute | solution.py:84
  213.0 13.1 %collective-permute-start.15 = (f16[128,2048]{1,0:T(8,128)(2,1)S(1)}, f16[128,2048]{1,0:T(8,128)(2,1)S(1)}, u32[]{:S(2)}, u32[]{:S(2)}) collective-permute-start(f16[128,2048]{1,0:T(8,128)(2,1)S(1)} %fusion.113), channel_id=1, source_target_pairs={{2,3},{1,0},{6,7},{5,4},{10,11},{9,8},{14,15},{13,12},{18,19},{17,... | collective-permute-start | bytes 1572872 | tf_op jit(solution)/shard_map/ppermute | solution.py:84
  226.0 16.1 %collective-permute-start.21 = (f16[128,2048]{1,0:T(8,128)(2,1)S(1)}, f16[128,2048]{1,0:T(8,128)(2,1)S(1)}, u32[]{:S(2)}, u32[]{:S(2)}) collective-permute-start(f16[128,2048]{1,0:T(8,128)(2,1)S(1)} %fusion.118), channel_id=1, source_target_pairs={{2,3},{1,0},{6,7},{5,4},{10,11},{9,8},{14,15},{13,12},{18,19},{17,... | collective-permute-start | bytes 1572872 | tf_op jit(solution)/shard_map/ppermute | solution.py:84
  238.3 23.8 %copy-start.1 = (f32[2,512]{1,0:T(2,128)S(1)}, f32[2,512]{1,0:T(2,128)}, u32[]{:S(2)}) copy-start(f32[2,512]{1,0:T(2,128)} %param.10) | copy-start | bytes 12292
  238.4 26.4 %copy-start = (f32[2,16,512]{2,1,0:T(8,128)S(1)}, f32[2,16,512]{2,1,0:T(8,128)}, u32[]{:S(2)}) copy-start(f32[2,16,512]{2,1,0:T(8,128)} %param.11) | copy-start | bytes 196612
  253.2 1.4 collective-permute-start.16
  253.3 2.9 %collective-permute-start.34 = (f32[2,16,2,512]{3,1,2,0:T(8,128)S(1)}, f32[2,16,2,512]{3,1,2,0:T(8,128)S(1)}, u32[]{:S(2)}, u32[]{:S(2)}) collective-permute-start(f32[2,16,2,512]{3,1,2,0:T(8,128)S(1)} %bitcast.240), channel_id=1, source_target_pairs={{0,4},{4,0},{8,12},{12,8},{1,5},{5,1},{9,13},{13,9},{2,6},{6,2},{1... | collective-permute-start | bytes 393224 | tf_op jit(solution)/shard_map/ppermute | solution.py:33
  254.6 4.5 %collective-permute-start.17 = (f32[1,16,2,512]{3,1,2,0:T(8,128)S(1)}, f32[1,16,2,512]{3,1,2,0:T(8,128)S(1)}, u32[]{:S(2)}, u32[]{:S(2)}) collective-permute-start(f32[1,16,2,512]{3,1,2,0:T(8,128)S(1)} %constant_dynamic-slice_fusion.3), channel_id=1, source_target_pairs={{0,8},{4,12},{8,0},{12,4},{1,9},{5,13},{9,1},{13,5},{2,10},{6,14},... | collective-permute-start | bytes 196616 | tf_op jit(solution)/shard_map/ppermute | solution.py:33
  256.2 4.6 %collective-permute-start.35 = (f32[1,16,2,512]{3,1,2,0:T(8,128)S(1)}, f32[1,16,2,512]{3,1,2,0:T(8,128)S(1)}, u32[]{:S(2)}, u32[]{:S(2)}) collective-permute-start(f32[1,16,2,512]{3,1,2,0:T(8,128)S(1)} %constant_dynamic-slice_fusion), channel_id=1, source_target_pairs={{0,8},{4,12},{8,0},{12,4},{1,9},{5,13},{9,1},{13,5},{2,10},{6,14},... | collective-permute-start | bytes 196616 | tf_op jit(solution)/shard_map/ppermute | solution.py:33
  259.2 4.0 %collective-permute-start.18 = (f32[1,16,512]{2,1,0:T(8,128)S(1)}, f32[1,16,512]{2,1,0:T(8,128)S(1)}, u32[]{:S(2)}, u32[]{:S(2)}) collective-permute-start(f32[1,16,512]{2,1,0:T(8,128)S(1)} %dynamic-slice_bitcast_fusion.1), channel_id=1, source_target_pairs={{0,16},{16,0},{1,17},{17,1},{2,18},{18,2},{3,19},{19,3},{4,20},{20... | collective-permute-start | bytes 98312 | tf_op jit(solution)/shard_map/ppermute | solution.py:33
  260.8 4.0 %collective-permute-start.36 = (f32[1,16,512]{2,1,0:T(8,128)S(1)}, f32[1,16,512]{2,1,0:T(8,128)S(1)}, u32[]{:S(2)}, u32[]{:S(2)}) collective-permute-start(f32[1,16,512]{2,1,0:T(8,128)S(1)} %dynamic-slice_bitcast_fusion), channel_id=1, source_target_pairs={{0,16},{16,0},{1,17},{17,1},{2,18},{18,2},{3,19},{19,3},{4,20},{20... | collective-permute-start | bytes 98312 | tf_op jit(solution)/shard_map/ppermute | solution.py:33
  265.0 4.3 %collective-permute-start.39 = (f32[2,16]{1,0:T(2,128)S(1)}, f32[2,16]{1,0:T(2,128)S(1)}, u32[]{:S(2)}, u32[]{:S(2)}) collective-permute-start(f32[2,16]{1,0:T(2,128)S(1)} %pad_maximum_fusion.2), channel_id=1, source_target_pairs={{0,1},{1,0},{2,3},{3,2},{4,5},{5,4},{6,7},{7,6},{8,9},{9,8},{10,11... | collective-permute-start | bytes 392 | tf_op jit(solution)/shard_map/ppermute | solution.py:44
  267.7 4.7 %collective-permute-start.37 = (f32[2,16]{1,0:T(2,128)S(1)}, f32[2,16]{1,0:T(2,128)S(1)}, u32[]{:S(2)}, u32[]{:S(2)}) collective-permute-start(f32[2,16]{1,0:T(2,128)S(1)} %pad_maximum_fusion.1), channel_id=1, source_target_pairs={{0,1},{1,0},{2,3},{3,2},{4,5},{5,4},{6,7},{7,6},{8,9},{9,8},{10,11... | collective-permute-start | bytes 392 | tf_op jit(solution)/shard_map/ppermute | solution.py:44
  269.3 4.6 %collective-permute-start.40 = (f32[2,16]{1,0:T(2,128)S(1)}, f32[2,16]{1,0:T(2,128)S(1)}, u32[]{:S(2)}, u32[]{:S(2)}) collective-permute-start(f32[2,16]{1,0:T(2,128)S(1)} %fusion.197), channel_id=1, source_target_pairs={{0,2},{1,3},{2,0},{3,1},{4,6},{5,7},{6,4},{7,5},{8,10},{9,11},{10,... | collective-permute-start | bytes 392 | tf_op jit(solution)/shard_map/ppermute | solution.py:44
  272.4 4.5 %collective-permute-start.38 = (f32[2,16]{1,0:T(2,128)S(1)}, f32[2,16]{1,0:T(2,128)S(1)}, u32[]{:S(2)}, u32[]{:S(2)}) collective-permute-start(f32[2,16]{1,0:T(2,128)S(1)} %fusion.198), channel_id=1, source_target_pairs={{0,2},{1,3},{2,0},{3,1},{4,6},{5,7},{6,4},{7,5},{8,10},{9,11},{10,... | collective-permute-start | bytes 392 | tf_op jit(solution)/shard_map/ppermute | solution.py:44

commit v2 on v1

v2 whole, which is shorter than its diff:
```python
import functools
import math

import jax
import jax.numpy as jnp
from jax import lax
from jax.experimental import pallas as pl
from jax.experimental.pallas import tpu as pltpu
from jax.sharding import PartitionSpec as P


RESID_MAX = 6.0
ENC_MAX = 0.125
F16_MAX = 65504.0
LAG = 3
VMEM_LIMIT = 20 << 20
WIDTHS = ((14, 12, 12, 14, 12), (12, 14, 12, 12, 14))


def chunk_list(layers, features):
    units = features // 64
    widths = WIDTHS if features % (64 * 128) == 0 and layers == 2 else ((16,) * 4,) * layers
    work = []
    for layer in range(layers):
        start = 0
        for width in widths[layer]:
            work.append((layer, start * units, (start + width) * units))
            start += width
    return work


def schedule(count):
    ops = [("work", 0)]
    for stage in range(count + LAG + 1):
        if stage < count + LAG:
            ops.append(("outer", stage))
        if 0 <= stage - 1 < count:
            ops.append(("inner", stage - 1))
        if stage + 1 < count or 0 <= stage - 1 - LAG < count:
            ops.append(("work", stage + 1))
    return ops


def work_kernel(enc_at, dec_at, pieces, scale, *refs):
    refs = list(refs)
    if enc_at is not None:
        rows_ref, enc_ref = refs[:2]
        del refs[:2]
    if dec_at is not None:
        base_ref, last_ref, bias_ref, dec_ref, sum_ref = refs[:5]
        del refs[:5]
    if enc_at is not None:
        pre_ref = refs.pop(0)
    if dec_at is not None:
        out_ref = refs.pop(0)
    if enc_at is not None:
        enc_buf, enc_sem = refs[:2]
        del refs[:2]
        layer, start, stop = enc_at
        enc_copy = pltpu.make_async_copy(
            enc_ref.at[layer, :, pl.ds(start, stop - start)], enc_buf, enc_sem
        )
        enc_copy.start()
    if dec_at is not None:
        act_ref, dec_buf, dec_sem = refs
        layer, start, stop = dec_at
        targets, tokens, _ = out_ref.shape
        depth = (stop - start) // pieces
        copies = []
        for m in range(targets):
            target = m + layer
            for piece in range(pieces):
                copy = pltpu.make_async_copy(
                    dec_ref.at[
                        target * (target + 1) // 2 + layer, pl.ds(start + piece * depth, depth)
                    ],
                    dec_buf.at[m * pieces + piece],
                    dec_sem.at[m * pieces + piece],
                )
                copy.start()
                copies.append(copy)
    if enc_at is not None:
        enc_copy.wait()
        pre_ref[...] = jnp.dot(rows_ref[0], enc_buf[...], preferred_element_type=jnp.float32)
    if dec_at is not None:
        bias = bias_ref[layer : layer + 1, start:stop] * scale
        act = jnp.maximum(base_ref[...] + last_ref[...] + bias, 0.0)
        high = act.astype(jnp.bfloat16)
        act_ref[:tokens] = high
        act_ref[tokens:] = (act - high.astype(jnp.float32)).astype(jnp.bfloat16)
        for m in range(targets):
            total = sum_ref[m]
            for piece in range(pieces):
                copies[m * pieces + piece].wait()
                weights = dec_buf[m * pieces + piece]
                high = weights.astype(jnp.bfloat16)
                low = (weights - high.astype(jnp.float32)).astype(jnp.bfloat16)
                part = act_ref[:, piece * depth : (piece + 1) * depth]
                both = jnp.dot(part, high, preferred_element_type=jnp.float32)
                rest = jnp.dot(part[:tokens], low, preferred_element_type=jnp.float32)
                total = total + (both[:tokens] + both[tokens:] + rest)
            out_ref[m] = total


def work_call(rows, enc_w, pre, bias, dec_w, sums, enc_at, dec_at, scale):
    operands, in_specs, out_specs, out_shape, scratch = [], [], [], [], []
    flops = moved = pieces = 0
    if enc_at is not None:
        layer, start, stop = enc_at
        _, tokens, width = rows.shape
        operands += [rows, pltpu.with_memory_space_constraint(enc_w, pltpu.HBM)]
        in_specs += [
            pl.BlockSpec((1, tokens, width), lambda i: (layer, 0, 0)),
            pl.BlockSpec(memory_space=pltpu.HBM),
        ]
        out_specs.append(pl.BlockSpec((tokens, stop - start), lambda i: (0, 0)))
        out_shape.append(jax.ShapeDtypeStruct((tokens, stop - start), jnp.float32))
        scratch += [
            pltpu.VMEM((width, stop - start), enc_w.dtype), pltpu.SemaphoreType.DMA,
        ]
        flops += 2 * tokens * width * (stop - start)
        moved += 2 * width * (stop - start)
    if dec_at is not None:
        _, low, high = dec_at
        targets, tokens, width = sums.shape
        pieces = 2 if (high - low) % 256 == 0 else 1
        operands += [*pre, bias, pltpu.with_memory_space_constraint(dec_w, pltpu.HBM), sums]
        in_specs += [
            pl.BlockSpec(pre[0].shape, lambda i: (0, 0)),
            pl.BlockSpec(pre[1].shape, lambda i: (0, 0)),
            pl.BlockSpec(bias.shape, lambda i: (0, 0)),
            pl.BlockSpec(memory_space=pltpu.HBM),
            pl.BlockSpec(sums.shape, lambda i: (0, 0, 0)),
        ]
        out_specs.append(pl.BlockSpec(sums.shape, lambda i: (0, 0, 0)))
        out_shape.append(jax.ShapeDtypeStruct(sums.shape, jnp.float32))
        scratch += [
            pltpu.VMEM((2 * tokens, high - low), jnp.bfloat16),
            pltpu.VMEM((targets * pieces, (high - low) // pieces, width), dec_w.dtype),
            pltpu.SemaphoreType.DMA((targets * pieces,)),
        ]
        flops += 6 * tokens * width * (high - low) * targets
        moved += 4 * width * (high - low) * targets
    outs = pl.pallas_call(
        functools.partial(work_kernel, enc_at, dec_at, pieces, scale),
        grid=(1,),
        in_specs=in_specs,
        out_specs=out_specs,
        out_shape=out_shape,
        scratch_shapes=scratch,
        compiler_params=pltpu.CompilerParams(vmem_limit_bytes=VMEM_LIMIT),
        cost_estimate=pl.CostEstimate(flops=flops, bytes_accessed=moved, transcendentals=0),
    )(*operands)
    return (outs[0] if enc_at is not None else None, outs[-1] if dec_at is not None else None)


def halving(rows, axis):
    size = lax.axis_size(axis)
    me = lax.axis_index(axis)
    bit = 1
    blocks = rows.reshape((size, rows.shape[0] // size) + rows.shape[1:])
    count = size
    while count > 1:
        pairs = blocks.reshape((count // 2, 2) + blocks.shape[1:])
        mine = (me // bit) % 2
        keep = lax.dynamic_index_in_dim(pairs, mine, 1, keepdims=False)
        give = lax.dynamic_index_in_dim(pairs, 1 - mine, 1, keepdims=False)
        got = lax.ppermute(give, axis, [(i, i ^ bit) for i in range(size)])
        blocks = keep + got
        bit *= 2
        count //= 2
    return blocks[0]


def butterfly(value, axis):
    size = lax.axis_size(axis)
    bit = 1
    while bit < size:
        value = value + lax.ppermute(value, axis, [(i, i ^ bit) for i in range(size)])
        bit *= 2
    return value


def gather_tokens(resid, axis):
    size = lax.axis_size(axis)
    if size != 2:
        return lax.all_gather(resid, axis, axis=1, tiled=True)
    other = lax.ppermute(resid, axis, [(0, 1), (1, 0)])
    first = lax.axis_index(axis) == 0
    return jnp.concatenate(
        [jnp.where(first, resid, other), jnp.where(first, other, resid)], axis=1
    )


def per_device(resid, enc_w, enc_b, dec_w, dec_b, target):
    layers, _, width = resid.shape
    features = enc_w.shape[2]
    size = lax.axis_size("width")
    scale = 2.0 ** math.floor(math.log2(F16_MAX / (width * size * RESID_MAX * ENC_MAX)))
    gathered = gather_tokens(resid, "layer") * jnp.asarray(scale, resid.dtype)
    tokens = gathered.shape[1]
    work = chunk_list(layers, features)
    place = lax.axis_index("width")
    outside = (place == 0) | (place == size - 1)
    partial, base, outer, inner = {}, {}, {}, {}
    sums = jnp.zeros((layers, tokens, dec_w.shape[2]), jnp.float32)
    recon = [None] * layers
    for kind, k in schedule(len(work)):
        if kind == "work":
            enc_at = work[k] if k < len(work) else None
            done = k - 2 - LAG
            dec_at = work[done] if 0 <= done < len(work) else None
            pre = None
            if dec_at is not None:
                last = jnp.where(
                    outside,
                    outer[done + LAG].astype(jnp.float32),
                    inner[done].astype(jnp.float32),
                )
                pre = (base[done], last)
            partial[k], new_sums = work_call(
                gathered, enc_w, pre, enc_b, dec_w, sums, enc_at, dec_at, scale
            )
            if dec_at is not None:
                layer, sums = dec_at[0], new_sums
                if done + 1 == len(work) or work[done + 1][0] > layer:
                    recon[layer] = sums[0]
                    sums = sums[1:]
        elif kind == "outer":
            pairs = []
            if k < len(work):
                pairs += [(0, 1), (3, 2)]
                value = partial[k]
            if k >= LAG:
                pairs += [(1, 0), (2, 3)]
                back = partial[k - LAG] + inner[k - LAG].astype(jnp.float32)
                value = jnp.where(outside, value, back) if k < len(work) else back
            outer[k] = lax.ppermute(value.astype(jnp.float16), "width", pairs)
        else:
            value = partial[k] + outer[k].astype(jnp.float32)
            base[k] = jnp.where(outside, partial[k], value)
            inner[k] = lax.ppermute(value.astype(jnp.float16), "width", [(1, 2), (2, 1)])

    outs, errs = [], []
    for m in range(layers):
        rows = recon[m].reshape(lax.axis_size("layer"), -1, recon[m].shape[1])
        rows = rows.transpose(1, 0, 2)
        rows = halving(rows, "feat").transpose(1, 0, 2)
        rows = halving(rows.reshape((-1,) + rows.shape[2:]), "layer")
        out = rows * (1.0 / scale) + dec_b[m]
        diff = out - target[m]
        sq = jnp.stack([jnp.sum(diff * diff, axis=1), jnp.sum(target[m] * target[m], axis=1)])
        sq = butterfly(sq, "width")
        outs.append(out)
        errs.append(sq[0] / (sq[1] + 1e-06))
    return jnp.stack(outs), jnp.stack(errs)


def solution(mesh):
    in_specs = (
        P(None, "layer", "width"),
        P(None, "width", ("layer", "feat")),
        P(None, ("layer", "feat")),
        P(None, ("layer", "feat"), "width"),
        P(None, "width"),
        P(None, ("layer", "feat"), "width"),
    )
    out_specs = (P(None, ("layer", "feat"), "width"), P(None, ("layer", "feat")))

    return jax.shard_map(
        per_device, mesh=mesh, in_specs=in_specs, out_specs=out_specs, check_vma=False
    )
```

time: 279 us -> 179 us (0.64)
  waiting for transfers between devices: 138 us -> 65.9 us
  matrix products: 65.9 us -> 0 us
  Pallas kernels: 0 us -> 49.6 us
  starting transfers between devices: 65.4 us -> 54.9 us
    ppermute x30 -> x23, waiting for transfers between devices: 125 us -> 54 us  [the longest x13 54 us: per_device(): outer[k] = lax.ppermute(value.astype(jnp.float16), 'width', pairs)]
    dot_general x25 -> x0, matrix products: 65.9 us -> none  [the longest x15 47.5 us: per_device(): jnp.dot(act, dec_w[block, lo:hi], precision=lax.Precision.HIGH, preferred...]
    pallas_call x0 -> x15, Pallas kernels: none -> 49.6 us  [work_call(): pl.pallas_call(functools.partial(work_kernel, enc_at, dec_at, pieces, sca...]
    ppermute x30 -> x23, starting transfers between devices: 50.7 us -> 41.1 us  [the longest x13 34 us: per_device(): outer[k] = lax.ppermute(value.astype(jnp.float16), 'width', pairs)]
    ppermute x4, waiting for transfers between devices: 5.21 us -> 2.42 us  [butterfly(): lax.ppermute(value, axis, [(i, i ^ bit) for i in range(size)])]
  transfers between devices with their start and end apart: 41 -> 34, of which waited for: 21 -> 17; matrix products, arithmetic and copies ran while one was open for 18% -> 2% of each run, Pallas kernels for 0% -> 25%
where the time goes in v2:
time: 179 us; the launch traced here: 178 us
  waiting for transfers between devices  65.9 us (37%)
  starting transfers between devices  54.9 us (31%)
  Pallas kernels  49.6 us (28%)
  other arithmetic  6.16 us (3%)
    ppermute x13, waiting for transfers between devices, per_device(): outer[k] = lax.ppermute(value.astype(jnp.float16), 'width', pairs)  54 us
    pallas_call x15, Pallas kernels, work_call(): pl.pallas_call(functools.partial(work_kernel, enc_at, dec_at, pieces, sca...  49.6 us
    ppermute x13, starting transfers between devices, per_device(): outer[k] = lax.ppermute(value.astype(jnp.float16), 'width', pairs)  34 us
    ppermute x10, starting transfers between devices, per_device(): lax.ppermute(value.astype(jnp.float16), 'width', [(1, 2), (2, 1)])  7.04 us
    ppermute x6, waiting for transfers between devices, halving(): got = lax.ppermute(give, axis, [(i, i ^ bit) for i in range(size)])  5.78 us
    ppermute x6, starting transfers between devices, halving(): got = lax.ppermute(give, axis, [(i, i ^ bit) for i in range(size)])  5.7 us
    ppermute x4, starting transfers between devices, butterfly(): lax.ppermute(value, axis, [(i, i ^ bit) for i in range(size)])  5.11 us
    ppermute x1, waiting for transfers between devices, gather_tokens(): other = lax.ppermute(resid, axis, [(0, 1), (1, 0)])  3.71 us
  transfers between devices with their start and end apart: 34, of which 17 were waited for; matrix products, arithmetic and copies ran while one was open for 2% of the time, Pallas kernels for 25%

profile of v2, /device:TPU:0, one launch (start us, length us, event | category | flops | bytes accessed | tf_op | source)
XLA Modules:
  0.0 178.2 jit_solution(17679176304937100388)
XLA Ops:
  0.6 3.1 %collective-permute-start = (bf16[2,64,512]{2,1,0:T(8,128)(2,1)}, bf16[2,64,512]{2,1,0:T(8,128)(2,1)S(1)}, u32[]{:S(2)}, u32[]{:S(2)}) collective-permute-start(bf16[2,64,512]{2,1,0:T(8,128)(2,1)} %param.6), channel_id=1, source_target_pairs={{0,16},{16,0},{1,17},{17,1},{2,18},{18,2},{3,19},{19,3},{4,20},{20... | collective-permute-start | bytes 393224 | tf_op jit(solution)/shard_map/ppermute | solution.py:188
  3.7 3.7 %collective-permute-done = bf16[2,64,512]{2,1,0:T(8,128)(2,1)S(1)} collective-permute-done((bf16[2,64,512]{2,1,0:T(8,128)(2,1)}, bf16[2,64,512]{2,1,0:T(8,128)(2,1)S(1)}, u32[]{:S(2)}, u32[]{:S(2)}) %collective-permute-start) | collective-permute-done | bytes 131104 | tf_op jit(solution)/shard_map/ppermute | solution.py:188
  7.4 0.9 broadcast_select_fusion.1
  8.4 1.8 %shard_map.78 = f32[128,1536]{1,0:T(8,128)S(1)} custom-call(bf16[2,128,512]{2,1,0:T(8,128)(2,1)S(1)} %maximum_multiply_fusion.refs_0_, bf16[2,512,8192]{2,1,0:T(8,128)(2,1)} %refs_1_.19), custom_call_target="tpu_custom_call" | custom-call | flops 201326592 | bytes 1572864 | tf_op jit(solution)/shard_map/pallas_call | solution.py:144
  10.3 3.7 %collective-permute-start.1 = (f16[128,1536]{1,0:T(8,128)(2,1)S(1)}, f16[128,1536]{1,0:T(8,128)(2,1)S(1)}, u32[]{:S(2)}, u32[]{:S(2)}) collective-permute-start(f16[128,1536]{1,0:T(8,128)(2,1)S(1)} %convert_element_type.155), channel_id=1, source_target_pairs={{0,1},{3,2},{4,5},{7,6},{8,9},{11,10},{12,13},{15,14},{16,17},{19,... | collective-permute-start | bytes 1179656 | tf_op jit(solution)/shard_map/ppermute | solution.py:238
  14.0 1.9 %shard_map.80 = f32[128,1792]{1,0:T(8,128)S(1)} custom-call(bf16[2,128,512]{2,1,0:T(8,128)(2,1)S(1)} %maximum_multiply_fusion.refs_0_, bf16[2,512,8192]{2,1,0:T(8,128)(2,1)} %refs_1_.19), custom_call_target="tpu_custom_call" | custom-call | flops 234881024 | bytes 1835008 | tf_op jit(solution)/shard_map/pallas_call | solution.py:144
  16.0 1.3 collective-permute-start.5
  17.3 1.8 %shard_map.79 = f32[128,1536]{1,0:T(8,128)S(1)} custom-call(bf16[2,128,512]{2,1,0:T(8,128)(2,1)S(1)} %maximum_multiply_fusion.refs_0_, bf16[2,512,8192]{2,1,0:T(8,128)(2,1)} %refs_1_.19), custom_call_target="tpu_custom_call" | custom-call | flops 201326592 | bytes 1572864 | tf_op jit(solution)/shard_map/pallas_call | solution.py:144
  19.2 1.3 collective-permute-start.4
  20.5 1.8 %shard_map.77 = f32[128,1536]{1,0:T(8,128)S(1)} custom-call(bf16[2,128,512]{2,1,0:T(8,128)(2,1)S(1)} %maximum_multiply_fusion.refs_0_, bf16[2,512,8192]{2,1,0:T(8,128)(2,1)} %refs_1_.19), custom_call_target="tpu_custom_call" | custom-call | flops 201326592 | bytes 1572864 | tf_op jit(solution)/shard_map/pallas_call | solution.py:144
  22.3 1.9 %shard_map.81 = f32[128,1792]{1,0:T(8,128)S(1)} custom-call(bf16[2,128,512]{2,1,0:T(8,128)(2,1)S(1)} %maximum_multiply_fusion.refs_0_, bf16[2,512,8192]{2,1,0:T(8,128)(2,1)} %refs_1_.19), custom_call_target="tpu_custom_call" | custom-call | flops 234881024 | bytes 1835008 | tf_op jit(solution)/shard_map/pallas_call | solution.py:144
  24.4 0.7 collective-permute-start.2
  25.1 8.2 %collective-permute-done.5 = f16[128,1792]{1,0:T(8,128)(2,1)S(1)} collective-permute-done((f16[128,1792]{1,0:T(8,128)(2,1)S(1)}, f16[128,1792]{1,0:T(8,128)(2,1)S(1)}, u32[]{:S(2)}, u32[]{:S(2)}) %collective-permute-start.5) | collective-permute-done | bytes 458784 | tf_op jit(solution)/shard_map/ppermute | solution.py:238
  33.4 0.7 collective-permute-start.6
  34.1 5.6 %collective-permute-done.4 = f16[128,1536]{1,0:T(8,128)(2,1)S(1)} collective-permute-done((f16[128,1536]{1,0:T(8,128)(2,1)S(1)}, f16[128,1536]{1,0:T(8,128)(2,1)S(1)}, u32[]{:S(2)}, u32[]{:S(2)}) %collective-permute-start.4) | collective-permute-done | bytes 393248 | tf_op jit(solution)/shard_map/ppermute | solution.py:238
  39.8 0.7 collective-permute-start.8
  40.7 7.3 %collective-permute-start.7 = (f16[128,1792]{1,0:T(8,128)(2,1)S(1)}, f16[128,1792]{1,0:T(8,128)(2,1)S(1)}, u32[]{:S(2)}, u32[]{:S(2)}) collective-permute-start(f16[128,1792]{1,0:T(8,128)(2,1)S(1)} %fusion.15), channel_id=1, source_target_pairs={{0,1},{3,2},{1,0},{2,3},{4,5},{7,6},{5,4},{6,7},{8,9},{11,10},{9,8... | collective-permute-start | bytes 1376264 | tf_op jit(solution)/shard_map/ppermute | solution.py:238
  48.2 10.6 %collective-permute-done.7 = f16[128,1792]{1,0:T(8,128)(2,1)S(1)} collective-permute-done((f16[128,1792]{1,0:T(8,128)(2,1)S(1)}, f16[128,1792]{1,0:T(8,128)(2,1)S(1)}, u32[]{:S(2)}, u32[]{:S(2)}) %collective-permute-start.7) | collective-permute-done | bytes 458784 | tf_op jit(solution)/shard_map/ppermute | solution.py:238
  59.1 6.0 %shard_map.82 = (f32[128,1536]{1,0:T(8,128)S(1)}, f32[2,128,512]{2,1,0:T(8,128)S(1)}) custom-call(bf16[2,128,512]{2,1,0:T(8,128)(2,1)S(1)} %maximum_multiply_fusion.refs_0_, bf16[2,512,8192]{2,1,0:T(8,128)(2,1)} %refs_1_.19, f32[128,1792]{1,0:T(8,128)S(1)} %get-tuple-element.33.refs_2_, f32[128,1792]{1,0:T(8,128)S(1)} %get-tuple-element.50.refs_3_, ...), custom_call_target="tpu_custom_call" | custom-call | flops 1610612736 | bytes 8912896 | tf_op jit(solution)/shard_map/pallas_call | solution.py:144
  65.2 1.8 %collective-permute-start.9 = (f16[128,1536]{1,0:T(8,128)(2,1)S(1)}, f16[128,1536]{1,0:T(8,128)(2,1)S(1)}, u32[]{:S(2)}, u32[]{:S(2)}) collective-permute-start(f16[128,1536]{1,0:T(8,128)(2,1)S(1)} %fusion.26), channel_id=1, source_target_pairs={{0,1},{3,2},{1,0},{2,3},{4,5},{7,6},{5,4},{6,7},{8,9},{11,10},{9,8... | collective-permute-start | bytes 1179656 | tf_op jit(solution)/shard_map/ppermute | solution.py:238
  67.3 0.7 collective-permute-start.10
  67.9 0.7 collective-permute-start.12
  68.6 5.3 %shard_map.83 = (f32[128,1792]{1,0:T(8,128)S(1)}, f32[2,128,512]{2,1,0:T(8,128)S(1)}) custom-call(bf16[2,128,512]{2,1,0:T(8,128)(2,1)S(1)} %maximum_multiply_fusion.refs_0_, bf16[2,512,8192]{2,1,0:T(8,128)(2,1)} %refs_1_.19, f32[128,1536]{1,0:T(8,128)S(1)} %get-tuple-element.42.refs_2_, f32[128,1536]{1,0:T(8,128)S(1)} %get-tuple-element.54.refs_3_, ...), custom_call_target="tpu_custom_call" | custom-call | flops 1442840576 | bytes 8126464 | tf_op jit(solution)/shard_map/pallas_call | solution.py:144
  74.0 0.2 fusion.8
  74.2 0.7 collective-permute-start.21
  74.9 5.3 %shard_map.84 = (f32[128,1536]{1,0:T(8,128)S(1)}, f32[2,128,512]{2,1,0:T(8,128)S(1)}) custom-call(bf16[2,128,512]{2,1,0:T(8,128)(2,1)S(1)} %maximum_multiply_fusion.refs_0_, bf16[2,512,8192]{2,1,0:T(8,128)(2,1)} %refs_1_.19, f32[128,1536]{1,0:T(8,128)S(1)} %get-tuple-element.45.refs_2_, f32[128,1536]{1,0:T(8,128)S(1)} %get-tuple-element.52.refs_3_, ...), custom_call_target="tpu_custom_call" | custom-call | flops 1409286144 | bytes 7864320 | tf_op jit(solution)/shard_map/pallas_call | solution.py:144
  80.3 8.1 %collective-permute-start.11 = (f16[128,1536]{1,0:T(8,128)(2,1)S(1)}, f16[128,1536]{1,0:T(8,128)(2,1)S(1)}, u32[]{:S(2)}, u32[]{:S(2)}) collective-permute-start(f16[128,1536]{1,0:T(8,128)(2,1)S(1)} %fusion.28), channel_id=1, source_target_pairs={{0,1},{3,2},{1,0},{2,3},{4,5},{7,6},{5,4},{6,7},{8,9},{11,10},{9,8... | collective-permute-start | bytes 1179656 | tf_op jit(solution)/shard_map/ppermute | solution.py:238
  88.7 5.5 %collective-permute-done.11 = f16[128,1536]{1,0:T(8,128)(2,1)S(1)} collective-permute-done((f16[128,1536]{1,0:T(8,128)(2,1)S(1)}, f16[128,1536]{1,0:T(8,128)(2,1)S(1)}, u32[]{:S(2)}, u32[]{:S(2)}) %collective-permute-start.11) | collective-permute-done | bytes 393248 | tf_op jit(solution)/shard_map/ppermute | solution.py:238
  94.5 0.9 collective-permute-start.25
  95.3 5.4 %collective-permute-done.13 = f16[128,1792]{1,0:T(8,128)(2,1)S(1)} collective-permute-done((f16[128,1792]{1,0:T(8,128)(2,1)S(1)}, f16[128,1792]{1,0:T(8,128)(2,1)S(1)}, u32[]{:S(2)}, u32[]{:S(2)}) %collective-permute-start.13) | collective-permute-done | bytes 458784 | tf_op jit(solution)/shard_map/ppermute | solution.py:238
  101.0 6.0 %shard_map.85 = (f32[128,1536]{1,0:T(8,128)S(1)}, f32[2,128,512]{2,1,0:T(8,128)S(1)}) custom-call(bf16[2,128,512]{2,1,0:T(8,128)(2,1)S(1)} %maximum_multiply_fusion.refs_0_, bf16[2,512,8192]{2,1,0:T(8,128)(2,1)} %refs_1_.19, f32[128,1792]{1,0:T(8,128)S(1)} %get-tuple-element.31.refs_2_, f32[128,1792]{1,0:T(8,128)S(1)} %get-tuple-element.49.refs_3_, ...), custom_call_target="tpu_custom_call" | custom-call | flops 1610612736 | bytes 8912896 | tf_op jit(solution)/shard_map/pallas_call | solution.py:144
  107.1 2.4 %collective-permute-start.22 = (f16[128,1536]{1,0:T(8,128)(2,1)S(1)}, f16[128,1536]{1,0:T(8,128)(2,1)S(1)}, u32[]{:S(2)}, u32[]{:S(2)}) collective-permute-start(f16[128,1536]{1,0:T(8,128)(2,1)S(1)} %fusion.30), channel_id=1, source_target_pairs={{0,1},{3,2},{1,0},{2,3},{4,5},{7,6},{5,4},{6,7},{8,9},{11,10},{9,8... | collective-permute-start | bytes 1179656 | tf_op jit(solution)/shard_map/ppermute | solution.py:238
  109.5 0.7 collective-permute-start.17
  110.2 5.3 %shard_map.86 = (f32[128,1792]{1,0:T(8,128)S(1)}, f32[2,128,512]{2,1,0:T(8,128)S(1)}) custom-call(bf16[2,128,512]{2,1,0:T(8,128)(2,1)S(1)} %maximum_multiply_fusion.refs_0_, bf16[2,512,8192]{2,1,0:T(8,128)(2,1)} %refs_1_.19, f32[128,1536]{1,0:T(8,128)S(1)} %get-tuple-element.41.refs_2_, f32[128,1536]{1,0:T(8,128)S(1)} %get-tuple-element.53.refs_3_, ...), custom_call_target="tpu_custom_call" | custom-call | flops 1442840576 | bytes 8126464 | tf_op jit(solution)/shard_map/pallas_call | solution.py:144
  115.6 1.3 collective-permute-start.26
  116.9 1.9 %collective-permute-done.22 = f16[128,1536]{1,0:T(8,128)(2,1)S(1)} collective-permute-done((f16[128,1536]{1,0:T(8,128)(2,1)S(1)}, f16[128,1536]{1,0:T(8,128)(2,1)S(1)}, u32[]{:S(2)}, u32[]{:S(2)}) %collective-permute-start.22) | collective-permute-done | bytes 393248 | tf_op jit(solution)/shard_map/ppermute | solution.py:238
  119.1 0.7 collective-permute-start.23
  119.7 2.4 %shard_map.87.refs_4_ = f32[1,128,512]{2,1,0:T(8,128)S(1)} custom-call(f32[128,1536]{1,0:T(8,128)S(1)} %get-tuple-element.34.refs_0_, f32[128,1536]{1,0:T(8,128)S(1)} %get-tuple-element.51.refs_1_, f32[2,8192]{1,0:T(2,128)S(1)} %copy-done, f32[3,8192,512]{2,1,0:T(8,128)} %refs_3_.9, f32[1,128,512]{2,1,0:T(8,128)S(1)} %get-tuple-element.47.refs_4_), custom_call_target="tpu_custom_call" | custom-call | flops 603979776 | bytes 3145728 | tf_op jit(solution)/shard_map/pallas_call | solution.py:144
  122.3 3.9 %collective-permute-start.18 = (f16[128,1792]{1,0:T(8,128)(2,1)S(1)}, f16[128,1792]{1,0:T(8,128)(2,1)S(1)}, u32[]{:S(2)}, u32[]{:S(2)}) collective-permute-start(f16[128,1792]{1,0:T(8,128)(2,1)S(1)} %fusion.19), channel_id=1, source_target_pairs={{0,1},{3,2},{1,0},{2,3},{4,5},{7,6},{5,4},{6,7},{8,9},{11,10},{9,8... | collective-permute-start | bytes 1376264 | tf_op jit(solution)/shard_map/ppermute | solution.py:238
  126.3 10.4 %collective-permute-done.18 = f16[128,1792]{1,0:T(8,128)(2,1)S(1)} collective-permute-done((f16[128,1792]{1,0:T(8,128)(2,1)S(1)}, f16[128,1792]{1,0:T(8,128)(2,1)S(1)}, u32[]{:S(2)}, u32[]{:S(2)}) %collective-permute-start.18) | collective-permute-done | bytes 458784 | tf_op jit(solution)/shard_map/ppermute | solution.py:238
  136.8 0.7 collective-permute-start.19
  137.6 1.3 collective-permute-start.24
  138.9 2.7 %shard_map.88.refs_4_ = f32[1,128,512]{2,1,0:T(8,128)S(1)} custom-call(f32[128,1792]{1,0:T(8,128)S(1)} %get-tuple-element.26.refs_0_, f32[128,1792]{1,0:T(8,128)S(1)} %get-tuple-element.48.refs_1_, f32[2,8192]{1,0:T(2,128)S(1)} %copy-done, f32[3,8192,512]{2,1,0:T(8,128)} %refs_3_.9, f32[1,128,512]{2,1,0:T(8,128)S(1)} %shard_map.87.refs_4_), custom_call_target="tpu_custom_call" | custom-call | flops 704643072 | bytes 3670016 | tf_op jit(solution)/shard_map/pallas_call | solution.py:144
  141.6 2.4 %shard_map.89.refs_4_ = f32[1,128,512]{2,1,0:T(8,128)S(1)} custom-call(f32[128,1536]{1,0:T(8,128)S(1)} %get-tuple-element.37.refs_0_, f32[128,1536]{1,0:T(8,128)S(1)} %convert_select_fusion.4.refs_1_, f32[2,8192]{1,0:T(2,128)S(1)} %copy-done, f32[3,8192,512]{2,1,0:T(8,128)} %refs_3_.9, f32[1,128,512]{2,1,0:T(8,128)S(1)} %shard_map.88.refs_4_), custom_call_target="tpu_custom_call" | custom-call | flops 603979776 | bytes 3145728 | tf_op jit(solution)/shard_map/pallas_call | solution.py:144
  144.1 1.5 collective-permute-start.20
  145.6 1.7 collective-permute-done.24
  147.4 2.4 %shard_map.90.refs_4_ = f32[1,128,512]{2,1,0:T(8,128)S(1)} custom-call(f32[128,1536]{1,0:T(8,128)S(1)} %get-tuple-element.39.refs_0_, f32[128,1536]{1,0:T(8,128)S(1)} %convert_select_fusion.5.refs_1_, f32[2,8192]{1,0:T(2,128)S(1)} %copy-done, f32[3,8192,512]{2,1,0:T(8,128)} %refs_3_.9, f32[1,128,512]{2,1,0:T(8,128)S(1)} %shard_map.89.refs_4_), custom_call_target="tpu_custom_call" | custom-call | flops 603979776 | bytes 3145728 | tf_op jit(solution)/shard_map/pallas_call | solution.py:144
  149.9 4.7 %collective-permute-done.20 = f16[128,1792]{1,0:T(8,128)(2,1)S(1)} collective-permute-done((f16[128,1792]{1,0:T(8,128)(2,1)S(1)}, f16[128,1792]{1,0:T(8,128)(2,1)S(1)}, u32[]{:S(2)}, u32[]{:S(2)}) %collective-permute-start.20) | collective-permute-done | bytes 458784 | tf_op jit(solution)/shard_map/ppermute | solution.py:238
  154.7 2.7 %shard_map.91 = f32[1,128,512]{2,1,0:T(8,128)S(1)} custom-call(f32[128,1792]{1,0:T(8,128)S(1)} %get-tuple-element.29.refs_0_, f32[128,1792]{1,0:T(8,128)S(1)} %convert_select_fusion.refs_1_, f32[2,8192]{1,0:T(2,128)S(1)} %copy-done, f32[3,8192,512]{2,1,0:T(8,128)} %refs_3_.9, f32[1,128,512]{2,1,0:T(8,128)S(1)} %shard_map.90.refs_4_), custom_call_target="tpu_custom_call" | custom-call | flops 704643072 | bytes 3670016 | tf_op jit(solution)/shard_map/pallas_call | solution.py:144
  157.6 0.5 collective-permute-start.27
  158.1 0.8 collective-permute-done.14
  158.9 1.6 collective-permute-start.15
  160.5 0.6 collective-permute-start.28
  161.1 2.3 %collective-permute-done.15 = f32[1,16,2,512]{3,1,2,0:T(8,128)S(1)} collective-permute-done((f32[1,16,2,512]{3,1,2,0:T(8,128)S(1)}, f32[1,16,2,512]{3,1,2,0:T(8,128)S(1)}, u32[]{:S(2)}, u32[]{:S(2)}) %collective-permute-start.15) | collective-permute-done | bytes 65568 | tf_op jit(solution)/shard_map/ppermute | solution.py:168
  163.4 1.7 collective-permute-start.16
  165.2 1.3 collective-permute-start.29
  166.5 1.0 collective-permute-done.16
  167.4 1.8 collective-permute-done.29
  169.4 2.0 %collective-permute-start.32 = (f32[2,16]{1,0:T(2,128)S(1)}, f32[2,16]{1,0:T(2,128)S(1)}, u32[]{:S(2)}, u32[]{:S(2)}) collective-permute-start(f32[2,16]{1,0:T(2,128)S(1)} %pad_maximum_fusion.2), channel_id=1, source_target_pairs={{0,1},{1,0},{2,3},{3,2},{4,5},{5,4},{6,7},{7,6},{8,9},{9,8},{10,11... | collective-permute-start | bytes 392 | tf_op jit(solution)/shard_map/ppermute | solution.py:179
  171.5 0.6 pad_maximum_fusion
  172.1 0.9 collective-permute-done.30
  173.1 3.0 %collective-permute-start.33 = (f32[2,16]{1,0:T(2,128)S(1)}, f32[2,16]{1,0:T(2,128)S(1)}, u32[]{:S(2)}, u32[]{:S(2)}) collective-permute-start(f32[2,16]{1,0:T(2,128)S(1)} %fusion.45), channel_id=1, source_target_pairs={{0,2},{1,3},{2,0},{3,1},{4,6},{5,7},{6,4},{7,5},{8,10},{9,11},{10,... | collective-permute-start | bytes 392 | tf_op jit(solution)/shard_map/ppermute | solution.py:179
  176.1 1.5 collective-permute-done.31
  177.7 0.6 pad_maximum_fusion.3
  (80 shorter events, 4.5 us)
Async XLA Ops:
  0.6 6.8 %collective-permute-start = (bf16[2,64,512]{2,1,0:T(8,128)(2,1)}, bf16[2,64,512]{2,1,0:T(8,128)(2,1)S(1)}, u32[]{:S(2)}, u32[]{:S(2)}) collective-permute-start(bf16[2,64,512]{2,1,0:T(8,128)(2,1)} %param.6), channel_id=1, source_target_pairs={{0,16},{16,0},{1,17},{17,1},{2,18},{18,2},{3,19},{19,3},{4,20},{20... | collective-permute-start | bytes 393224 | tf_op jit(solution)/shard_map/ppermute | solution.py:188
  10.2 48.9 %copy-start = (f32[2,8192]{1,0:T(2,128)S(1)}, f32[2,8192]{1,0:T(2,128)}, u32[]{:S(2)}) copy-start(f32[2,8192]{1,0:T(2,128)} %refs_2_.9) | copy-start | bytes 196612
  10.3 14.0 %collective-permute-start.1 = (f16[128,1536]{1,0:T(8,128)(2,1)S(1)}, f16[128,1536]{1,0:T(8,128)(2,1)S(1)}, u32[]{:S(2)}, u32[]{:S(2)}) collective-permute-start(f16[128,1536]{1,0:T(8,128)(2,1)S(1)} %convert_element_type.155), channel_id=1, source_target_pairs={{0,1},{3,2},{4,5},{7,6},{8,9},{11,10},{12,13},{15,14},{16,17},{19,... | collective-permute-start | bytes 1179656 | tf_op jit(solution)/shard_map/ppermute | solution.py:238
  16.0 17.3 %collective-permute-start.5 = (f16[128,1792]{1,0:T(8,128)(2,1)S(1)}, f16[128,1792]{1,0:T(8,128)(2,1)S(1)}, u32[]{:S(2)}, u32[]{:S(2)}) collective-permute-start(f16[128,1792]{1,0:T(8,128)(2,1)S(1)} %convert_element_type.163), channel_id=1, source_target_pairs={{0,1},{3,2},{4,5},{7,6},{8,9},{11,10},{12,13},{15,14},{16,17},{19,... | collective-permute-start | bytes 1376264 | tf_op jit(solution)/shard_map/ppermute | solution.py:238
  19.2 20.5 %collective-permute-start.4 = (f16[128,1536]{1,0:T(8,128)(2,1)S(1)}, f16[128,1536]{1,0:T(8,128)(2,1)S(1)}, u32[]{:S(2)}, u32[]{:S(2)}) collective-permute-start(f16[128,1536]{1,0:T(8,128)(2,1)S(1)} %convert_element_type.161), channel_id=1, source_target_pairs={{0,1},{3,2},{4,5},{7,6},{8,9},{11,10},{12,13},{15,14},{16,17},{19,... | collective-permute-start | bytes 1179656 | tf_op jit(solution)/shard_map/ppermute | solution.py:238
  24.4 23.6 %collective-permute-start.2 = (f16[128,1536]{1,0:T(8,128)(2,1)S(1)}, f16[128,1536]{1,0:T(8,128)(2,1)S(1)}, u32[]{:S(2)}, u32[]{:S(2)}) collective-permute-start(f16[128,1536]{1,0:T(8,128)(2,1)S(1)} %get-tuple-element.43), channel_id=1, source_target_pairs={{1,2},{2,1},{5,6},{6,5},{9,10},{10,9},{13,14},{14,13},{17,18},{18,... | collective-permute-start | bytes 1179656 | tf_op jit(solution)/shard_map/ppermute | solution.py:242
  33.4 7.1 %collective-permute-start.6 = (f16[128,1792]{1,0:T(8,128)(2,1)S(1)}, f16[128,1792]{1,0:T(8,128)(2,1)S(1)}, u32[]{:S(2)}, u32[]{:S(2)}) collective-permute-start(f16[128,1792]{1,0:T(8,128)(2,1)S(1)} %get-tuple-element.32), channel_id=1, source_target_pairs={{1,2},{2,1},{5,6},{6,5},{9,10},{10,9},{13,14},{14,13},{17,18},{18,... | collective-permute-start | bytes 1376264 | tf_op jit(solution)/shard_map/ppermute | solution.py:242
  39.8 25.2 %collective-permute-start.8 = (f16[128,1536]{1,0:T(8,128)(2,1)S(1)}, f16[128,1536]{1,0:T(8,128)(2,1)S(1)}, u32[]{:S(2)}, u32[]{:S(2)}) collective-permute-start(f16[128,1536]{1,0:T(8,128)(2,1)S(1)} %get-tuple-element.44), channel_id=1, source_target_pairs={{1,2},{2,1},{5,6},{6,5},{9,10},{10,9},{13,14},{14,13},{17,18},{18,... | collective-permute-start | bytes 1179656 | tf_op jit(solution)/shard_map/ppermute | solution.py:242
  40.7 18.1 %collective-permute-start.7 = (f16[128,1792]{1,0:T(8,128)(2,1)S(1)}, f16[128,1792]{1,0:T(8,128)(2,1)S(1)}, u32[]{:S(2)}, u32[]{:S(2)}) collective-permute-start(f16[128,1792]{1,0:T(8,128)(2,1)S(1)} %fusion.15), channel_id=1, source_target_pairs={{0,1},{3,2},{1,0},{2,3},{4,5},{7,6},{5,4},{6,7},{8,9},{11,10},{9,8... | collective-permute-start | bytes 1376264 | tf_op jit(solution)/shard_map/ppermute | solution.py:238
  48.1 18.9 %collective-permute-start.3 = (f16[128,1536]{1,0:T(8,128)(2,1)S(1)}, f16[128,1536]{1,0:T(8,128)(2,1)S(1)}, u32[]{:S(2)}, u32[]{:S(2)}) collective-permute-start(f16[128,1536]{1,0:T(8,128)(2,1)S(1)} %fusion.24), channel_id=1, source_target_pairs={{0,1},{3,2},{1,0},{2,3},{4,5},{7,6},{5,4},{6,7},{8,9},{11,10},{9,8... | collective-permute-start | bytes 1179656 | tf_op jit(solution)/shard_map/ppermute | solution.py:238
  65.2 8.8 %collective-permute-start.9 = (f16[128,1536]{1,0:T(8,128)(2,1)S(1)}, f16[128,1536]{1,0:T(8,128)(2,1)S(1)}, u32[]{:S(2)}, u32[]{:S(2)}) collective-permute-start(f16[128,1536]{1,0:T(8,128)(2,1)S(1)} %fusion.26), channel_id=1, source_target_pairs={{0,1},{3,2},{1,0},{2,3},{4,5},{7,6},{5,4},{6,7},{8,9},{11,10},{9,8... | collective-permute-start | bytes 1179656 | tf_op jit(solution)/shard_map/ppermute | solution.py:238
  67.3 12.9 %collective-permute-start.10 = (f16[128,1536]{1,0:T(8,128)(2,1)S(1)}, f16[128,1536]{1,0:T(8,128)(2,1)S(1)}, u32[]{:S(2)}, u32[]{:S(2)}) collective-permute-start(f16[128,1536]{1,0:T(8,128)(2,1)S(1)} %get-tuple-element.40), channel_id=1, source_target_pairs={{1,2},{2,1},{5,6},{6,5},{9,10},{10,9},{13,14},{14,13},{17,18},{18,... | collective-permute-start | bytes 1179656 | tf_op jit(solution)/shard_map/ppermute | solution.py:242
  67.9 20.5 %collective-permute-start.12 = (f16[128,1792]{1,0:T(8,128)(2,1)S(1)}, f16[128,1792]{1,0:T(8,128)(2,1)S(1)}, u32[]{:S(2)}, u32[]{:S(2)}) collective-permute-start(f16[128,1792]{1,0:T(8,128)(2,1)S(1)} %get-tuple-element.30), channel_id=1, source_target_pairs={{1,2},{2,1},{5,6},{6,5},{9,10},{10,9},{13,14},{14,13},{17,18},{18,... | collective-permute-start | bytes 1376264 | tf_op jit(solution)/shard_map/ppermute | solution.py:242
  74.2 32.7 %collective-permute-start.21 = (f16[128,1536]{1,0:T(8,128)(2,1)S(1)}, f16[128,1536]{1,0:T(8,128)(2,1)S(1)}, u32[]{:S(2)}, u32[]{:S(2)}) collective-permute-start(f16[128,1536]{1,0:T(8,128)(2,1)S(1)} %get-tuple-element.35), channel_id=1, source_target_pairs={{1,2},{2,1},{5,6},{6,5},{9,10},{10,9},{13,14},{14,13},{17,18},{18,... | collective-permute-start | bytes 1179656 | tf_op jit(solution)/shard_map/ppermute | solution.py:242
  80.3 13.9 %collective-permute-start.11 = (f16[128,1536]{1,0:T(8,128)(2,1)S(1)}, f16[128,1536]{1,0:T(8,128)(2,1)S(1)}, u32[]{:S(2)}, u32[]{:S(2)}) collective-permute-start(f16[128,1536]{1,0:T(8,128)(2,1)S(1)} %fusion.28), channel_id=1, source_target_pairs={{0,1},{3,2},{1,0},{2,3},{4,5},{7,6},{5,4},{6,7},{8,9},{11,10},{9,8... | collective-permute-start | bytes 1179656 | tf_op jit(solution)/shard_map/ppermute | solution.py:238
  88.6 12.2 %collective-permute-start.13 = (f16[128,1792]{1,0:T(8,128)(2,1)S(1)}, f16[128,1792]{1,0:T(8,128)(2,1)S(1)}, u32[]{:S(2)}, u32[]{:S(2)}) collective-permute-start(f16[128,1792]{1,0:T(8,128)(2,1)S(1)} %fusion.17), channel_id=1, source_target_pairs={{0,1},{3,2},{1,0},{2,3},{4,5},{7,6},{5,4},{6,7},{8,9},{11,10},{9,8... | collective-permute-start | bytes 1376264 | tf_op jit(solution)/shard_map/ppermute | solution.py:238
  94.5 21.1 %collective-permute-start.25 = (f16[128,1536]{1,0:T(8,128)(2,1)S(1)}, f16[128,1536]{1,0:T(8,128)(2,1)S(1)}, u32[]{:S(2)}, u32[]{:S(2)}) collective-permute-start(f16[128,1536]{1,0:T(8,128)(2,1)S(1)} %get-tuple-element.36), channel_id=1, source_target_pairs={{1,2},{2,1},{5,6},{6,5},{9,10},{10,9},{13,14},{14,13},{17,18},{18,... | collective-permute-start | bytes 1179656 | tf_op jit(solution)/shard_map/ppermute | solution.py:242
  107.1 11.7 %collective-permute-start.22 = (f16[128,1536]{1,0:T(8,128)(2,1)S(1)}, f16[128,1536]{1,0:T(8,128)(2,1)S(1)}, u32[]{:S(2)}, u32[]{:S(2)}) collective-permute-start(f16[128,1536]{1,0:T(8,128)(2,1)S(1)} %fusion.30), channel_id=1, source_target_pairs={{0,1},{3,2},{1,0},{2,3},{4,5},{7,6},{5,4},{6,7},{8,9},{11,10},{9,8... | collective-permute-start | bytes 1179656 | tf_op jit(solution)/shard_map/ppermute | solution.py:238
  109.5 12.7 %collective-permute-start.17 = (f16[128,1792]{1,0:T(8,128)(2,1)S(1)}, f16[128,1792]{1,0:T(8,128)(2,1)S(1)}, u32[]{:S(2)}, u32[]{:S(2)}) collective-permute-start(f16[128,1792]{1,0:T(8,128)(2,1)S(1)} %get-tuple-element.27), channel_id=1, source_target_pairs={{1,2},{2,1},{5,6},{6,5},{9,10},{10,9},{13,14},{14,13},{17,18},{18,... | collective-permute-start | bytes 1376264 | tf_op jit(solution)/shard_map/ppermute | solution.py:242
  115.6 10.5 %collective-permute-start.26 = (f16[128,1536]{1,0:T(8,128)(2,1)S(1)}, f16[128,1536]{1,0:T(8,128)(2,1)S(1)}, u32[]{:S(2)}, u32[]{:S(2)}) collective-permute-start(f16[128,1536]{1,0:T(8,128)(2,1)S(1)} %fusion.32), channel_id=1, source_target_pairs={{1,0},{2,3},{5,4},{6,7},{9,8},{10,11},{13,12},{14,15},{17,16},{18,... | collective-permute-start | bytes 1179656 | tf_op jit(solution)/shard_map/ppermute | solution.py:238
  119.1 18.5 %collective-permute-start.23 = (f16[128,1536]{1,0:T(8,128)(2,1)S(1)}, f16[128,1536]{1,0:T(8,128)(2,1)S(1)}, u32[]{:S(2)}, u32[]{:S(2)}) collective-permute-start(f16[128,1536]{1,0:T(8,128)(2,1)S(1)} %get-tuple-element.38), channel_id=1, source_target_pairs={{1,2},{2,1},{5,6},{6,5},{9,10},{10,9},{13,14},{14,13},{17,18},{18,... | collective-permute-start | bytes 1179656 | tf_op jit(solution)/shard_map/ppermute | solution.py:242
  122.3 14.3 %collective-permute-start.18 = (f16[128,1792]{1,0:T(8,128)(2,1)S(1)}, f16[128,1792]{1,0:T(8,128)(2,1)S(1)}, u32[]{:S(2)}, u32[]{:S(2)}) collective-permute-start(f16[128,1792]{1,0:T(8,128)(2,1)S(1)} %fusion.19), channel_id=1, source_target_pairs={{0,1},{3,2},{1,0},{2,3},{4,5},{7,6},{5,4},{6,7},{8,9},{11,10},{9,8... | collective-permute-start | bytes 1376264 | tf_op jit(solution)/shard_map/ppermute | solution.py:238
  136.8 7.2 %collective-permute-start.19 = (f16[128,1792]{1,0:T(8,128)(2,1)S(1)}, f16[128,1792]{1,0:T(8,128)(2,1)S(1)}, u32[]{:S(2)}, u32[]{:S(2)}) collective-permute-start(f16[128,1792]{1,0:T(8,128)(2,1)S(1)} %get-tuple-element.28), channel_id=1, source_target_pairs={{1,2},{2,1},{5,6},{6,5},{9,10},{10,9},{13,14},{14,13},{17,18},{18,... | collective-permute-start | bytes 1376264 | tf_op jit(solution)/shard_map/ppermute | solution.py:242
  137.6 9.7 %collective-permute-start.24 = (f16[128,1536]{1,0:T(8,128)(2,1)S(1)}, f16[128,1536]{1,0:T(8,128)(2,1)S(1)}, u32[]{:S(2)}, u32[]{:S(2)}) collective-permute-start(f16[128,1536]{1,0:T(8,128)(2,1)S(1)} %fusion.31), channel_id=1, source_target_pairs={{1,0},{2,3},{5,4},{6,7},{9,8},{10,11},{13,12},{14,15},{17,16},{18,... | collective-permute-start | bytes 1179656 | tf_op jit(solution)/shard_map/ppermute | solution.py:238
  144.1 10.5 %collective-permute-start.20 = (f16[128,1792]{1,0:T(8,128)(2,1)S(1)}, f16[128,1792]{1,0:T(8,128)(2,1)S(1)}, u32[]{:S(2)}, u32[]{:S(2)}) collective-permute-start(f16[128,1792]{1,0:T(8,128)(2,1)S(1)} %fusion.20), channel_id=1, source_target_pairs={{1,0},{2,3},{5,4},{6,7},{9,8},{10,11},{13,12},{14,15},{17,16},{18,... | collective-permute-start | bytes 1376264 | tf_op jit(solution)/shard_map/ppermute | solution.py:238
  147.4 19.0 %copy-start.2 = (f32[2,512]{1,0:T(2,128)S(1)}, f32[2,512]{1,0:T(2,128)}, u32[]{:S(2)}) copy-start(f32[2,512]{1,0:T(2,128)} %param.10) | copy-start | bytes 12292
  147.4 21.8 %copy-start.1 = (f32[2,16,512]{2,1,0:T(8,128)S(1)}, f32[2,16,512]{2,1,0:T(8,128)}, u32[]{:S(2)}) copy-start(f32[2,16,512]{2,1,0:T(8,128)} %param.11) | copy-start | bytes 196612
  157.4 1.4 collective-permute-start.14
  157.6 2.9 %collective-permute-start.27 = (f32[2,16,2,512]{3,1,2,0:T(8,128)S(1)}, f32[2,16,2,512]{3,1,2,0:T(8,128)S(1)}, u32[]{:S(2)}, u32[]{:S(2)}) collective-permute-start(f32[2,16,2,512]{3,1,2,0:T(8,128)S(1)} %bitcast.75), channel_id=1, source_target_pairs={{0,4},{4,0},{8,12},{12,8},{1,5},{5,1},{9,13},{13,9},{2,6},{6,2},{1... | collective-permute-start | bytes 393224 | tf_op jit(solution)/shard_map/ppermute | solution.py:168
  158.9 4.5 %collective-permute-start.15 = (f32[1,16,2,512]{3,1,2,0:T(8,128)S(1)}, f32[1,16,2,512]{3,1,2,0:T(8,128)S(1)}, u32[]{:S(2)}, u32[]{:S(2)}) collective-permute-start(f32[1,16,2,512]{3,1,2,0:T(8,128)S(1)} %constant_dynamic-slice_fusion.3), channel_id=1, source_target_pairs={{0,8},{4,12},{8,0},{12,4},{1,9},{5,13},{9,1},{13,5},{2,10},{6,14},... | collective-permute-start | bytes 196616 | tf_op jit(solution)/shard_map/ppermute | solution.py:168
  160.5 4.6 %collective-permute-start.28 = (f32[1,16,2,512]{3,1,2,0:T(8,128)S(1)}, f32[1,16,2,512]{3,1,2,0:T(8,128)S(1)}, u32[]{:S(2)}, u32[]{:S(2)}) collective-permute-start(f32[1,16,2,512]{3,1,2,0:T(8,128)S(1)} %constant_dynamic-slice_fusion), channel_id=1, source_target_pairs={{0,8},{4,12},{8,0},{12,4},{1,9},{5,13},{9,1},{13,5},{2,10},{6,14},... | collective-permute-start | bytes 196616 | tf_op jit(solution)/shard_map/ppermute | solution.py:168
  163.4 4.0 %collective-permute-start.16 = (f32[1,16,512]{2,1,0:T(8,128)S(1)}, f32[1,16,512]{2,1,0:T(8,128)S(1)}, u32[]{:S(2)}, u32[]{:S(2)}) collective-permute-start(f32[1,16,512]{2,1,0:T(8,128)S(1)} %dynamic-slice_bitcast_fusion.1), channel_id=1, source_target_pairs={{0,16},{16,0},{1,17},{17,1},{2,18},{18,2},{3,19},{19,3},{4,20},{20... | collective-permute-start | bytes 98312 | tf_op jit(solution)/shard_map/ppermute | solution.py:168
  165.2 4.0 %collective-permute-start.29 = (f32[1,16,512]{2,1,0:T(8,128)S(1)}, f32[1,16,512]{2,1,0:T(8,128)S(1)}, u32[]{:S(2)}, u32[]{:S(2)}) collective-permute-start(f32[1,16,512]{2,1,0:T(8,128)S(1)} %dynamic-slice_bitcast_fusion), channel_id=1, source_target_pairs={{0,16},{16,0},{1,17},{17,1},{2,18},{18,2},{3,19},{19,3},{4,20},{20... | collective-permute-start | bytes 98312 | tf_op jit(solution)/shard_map/ppermute | solution.py:168
  169.3 3.6 %collective-permute-start.30 = (f32[2,16]{1,0:T(2,128)S(1)}, f32[2,16]{1,0:T(2,128)S(1)}, u32[]{:S(2)}, u32[]{:S(2)}) collective-permute-start(f32[2,16]{1,0:T(2,128)S(1)} %pad_maximum_fusion.1), channel_id=1, source_target_pairs={{0,1},{1,0},{2,3},{3,2},{4,5},{5,4},{6,7},{7,6},{8,9},{9,8},{10,11... | collective-permute-start | bytes 392 | tf_op jit(solution)/shard_map/ppermute | solution.py:179
  169.4 3.6 %collective-permute-start.32 = (f32[2,16]{1,0:T(2,128)S(1)}, f32[2,16]{1,0:T(2,128)S(1)}, u32[]{:S(2)}, u32[]{:S(2)}) collective-permute-start(f32[2,16]{1,0:T(2,128)S(1)} %pad_maximum_fusion.2), channel_id=1, source_target_pairs={{0,1},{1,0},{2,3},{3,2},{4,5},{5,4},{6,7},{7,6},{8,9},{9,8},{10,11... | collective-permute-start | bytes 392 | tf_op jit(solution)/shard_map/ppermute | solution.py:179
  173.0 4.5 %collective-permute-start.31 = (f32[2,16]{1,0:T(2,128)S(1)}, f32[2,16]{1,0:T(2,128)S(1)}, u32[]{:S(2)}, u32[]{:S(2)}) collective-permute-start(f32[2,16]{1,0:T(2,128)S(1)} %fusion.46), channel_id=1, source_target_pairs={{0,2},{1,3},{2,0},{3,1},{4,6},{5,7},{6,4},{7,5},{8,10},{9,11},{10,... | collective-permute-start | bytes 392 | tf_op jit(solution)/shard_map/ppermute | solution.py:179
  173.1 4.5 %collective-permute-start.33 = (f32[2,16]{1,0:T(2,128)S(1)}, f32[2,16]{1,0:T(2,128)S(1)}, u32[]{:S(2)}, u32[]{:S(2)}) collective-permute-start(f32[2,16]{1,0:T(2,128)S(1)} %fusion.45), channel_id=1, source_target_pairs={{0,2},{1,3},{2,0},{3,1},{4,6},{5,7},{6,4},{7,5},{8,10},{9,11},{10,... | collective-permute-start | bytes 392 | tf_op jit(solution)/shard_map/ppermute | solution.py:179
